TPU v7x, 32 devices: a whole 2x2x4 slice. The times are simulated.
32 devices in a mesh: dp: 8 (over y, x, core), chan: 4 (over z).
Axes of the slice: x: 2, y: 2, z: 4, core: 2. Of those that a mesh axis runs over, the one named last changes fastest.
Arguments:
- patches: bfloat16 [64, 256, 1280], P('dp', None, 'chan'), may hold values from -13 to 13
- cotangent: bfloat16 [64, 256, 1280], P('dp', None, 'chan'), may hold values from -33 to 33
- w_token_in: bfloat16 [640, 256], replicated, may hold values from -0.375 to 0.375
- b_token_in: float32 [640], replicated, may hold values from -3 to 3
- w_token_out: bfloat16 [256, 640], replicated, may hold values from -0.25 to 0.25
- layer_norm_gain: float32 [1280], replicated, may hold values from 0.25 to 1.75
- layer_norm_bias: float32 [1280], replicated, may hold values from -3 to 3
Outputs:
- grad_patches: bfloat16 [64, 256, 1280], P('dp', None, 'chan')
- grad_w_in: float32 [640, 256], replicated
- grad_w_out: float32 [256, 640], replicated
- grad_b_in: float32 [640], replicated
- grad_gain: float32 [1280], P('chan')
- grad_shift: float32 [1280], P('chan')
All inputs are finite; a program needn't handle non-finite values.
Results may differ from a plain program's by a relative error of at most 0.0065.
Values may be sent and summed in bfloat16 or wider, within the bound.
No kernel may reach another device: no remote copies, remote signals or barrier semaphores. Data moves between devices by JAX's collectives and lax.ppermute only.
A program may use at most 64 MiB of HBM per device.

v0:
```python
import functools
import math

import jax
import jax.numpy as jnp
from jax import lax
from jax.experimental import pallas as pl
from jax.experimental.pallas import tpu as pltpu
from jax.sharding import PartitionSpec as P


eps_norm = 1e-05
STEP = 32
SPREAD = 4 << 30
EXTRA = 16
F32 = jnp.float32
BF16 = jnp.bfloat16
VM = pl.BlockSpec(memory_space=pltpu.VMEM)
LIMIT = pltpu.CompilerParams(vmem_limit_bytes=24 << 20)


def call(body, outs, args, flops=0):
    nbytes = sum(a.size * a.dtype.itemsize for a in (*args, *outs))
    return pl.pallas_call(
        body,
        out_shape=outs,
        in_specs=[VM] * len(args),
        out_specs=[VM] * len(outs),
        compiler_params=LIMIT,
        cost_estimate=pl.CostEstimate(
            flops=flops, bytes_accessed=nbytes, transcendentals=0
        ),
    )(*args)


def shape(dims, dtype=F32):
    return jax.ShapeDtypeStruct(tuple(dims), dtype)


def dot(a, b, ca, cb, precision=None):
    return lax.dot_general(
        a, b, (((ca,), (cb,)), ((), ())), precision=precision, preferred_element_type=F32
    )


def high_low(v):
    high = v.astype(BF16)
    return high, (v - high.astype(F32)).astype(BF16)


def tree(values):
    values = list(values)
    while len(values) > 1:
        values = [a + b for a, b in zip(values[::2], values[1::2], strict=True)]
    return values[0]


def radices_of(n):
    factors, left = [2], n // 2
    while left > 1:
        r = 4 if left % 4 == 0 else 2
        factors.append(r)
        left //= r
    assert math.prod(factors) == n
    return factors


def exchange(value, axis, n, stride, radix):
    got = []
    for j in range(1, radix):
        got.append(lax.ppermute(value, axis, [(i, i ^ (j * stride)) for i in range(n)]))
    return got


def exchange_each(values, axis, n, stride):
    return [
        lax.ppermute(v, axis, [(i, i ^ (j * stride)) for i in range(n)])
        for j, v in enumerate(values, 1)
    ]


def tiny_rows(row, extra=EXTRA):
    high, low = high_low(row)
    return jnp.concatenate([high, low, jnp.zeros((extra - 2, row.shape[1]), BF16)], axis=0)


def join_pair(block):
    return block[0:1].astype(F32) + block[1:2].astype(F32)


def stats_body(x_ref, o_ref):
    images = x_ref.shape[0]
    for b in range(images):
        x = x_ref[b].astype(F32)
        o_ref[b : b + 1, :] = jnp.sum(x, axis=0, keepdims=True)
        o_ref[images + b : images + b + 1, :] = jnp.sum(x * x, axis=0, keepdims=True)


def spread_body(n_chan, patches, gain_ref, bias_ref, gain_o, bias_o):
    width = gain_o.shape[0]
    where = lax.axis_index("chan")
    for i in range(n_chan):

        @pl.when(where == i)
        def _():
            for src, dst in ((gain_ref, gain_o), (bias_ref, bias_o)):
                row = src[0:1, i * width : (i + 1) * width]
                rows = jnp.broadcast_to(row, (patches, width))
                dst[...] = jnp.transpose(rows, (1, 0))


def main_body(n_parts, channels, x_ref, *refs):
    parts = refs[:n_parts]
    gain_ref, bias_ref, w_ref, b_ref, cot_ref, w_out_ref = refs[n_parts : n_parts + 6]
    mr_ref, n_ref, act_ref, gp_ref, gn_ref, db_ref, *work_refs, acc_ref = refs[n_parts + 6 :]
    pre_refs, ga_refs = work_refs[:2], work_refs[2:]
    images, width, _ = x_ref.shape
    totals = tree([p[...] for p in parts]) / channels
    mean = totals[:images]
    rstd = lax.rsqrt(totals[images:] - mean * mean + eps_norm)
    mr_ref[0] = mean
    mr_ref[1] = rstd
    acc_ref[...] = jnp.zeros_like(acc_ref)
    step = STEP

    def project(b):
        xhat = (x_ref[b].astype(F32) - mr_ref[0, b : b + 1, :]) * mr_ref[1, b : b + 1, :]
        normed = (xhat * gain_ref[...] + bias_ref[...]).astype(BF16)
        n_ref[b] = normed
        pre_refs[b % 2][...] = dot(normed, w_ref[...], 1, 1)
        ga_refs[b % 2][...] = dot(cot_ref[b], w_out_ref[...], 1, 0)

    def back(b):
        gn_ref[b] = (0.5 * dot(gp_ref[b], w_ref[...], 1, 0)).astype(BF16)

    def gelu(b):
        for r in range(0, width, step):
            rows = slice(r, r + step)
            pre = pre_refs[b % 2][rows, :] + b_ref[...]
            twice = 1.0 + lax.erf(pre * (1.0 / math.sqrt(2.0)))
            act_ref[b, rows, :] = (pre * twice).astype(BF16)
            bell = jnp.exp2((pre * pre) * (-0.5 / math.log(2.0)))
            slope = twice + (pre * math.sqrt(2.0 / math.pi)) * bell
            gp = (ga_refs[b % 2][rows, :] * slope).astype(BF16)
            gp_ref[b, rows, :] = gp
            gpf = gp.astype(F32)
            acc_ref[...] += functools.reduce(
                jnp.add, [gpf[i : i + 8] for i in range(0, step, 8)]
            )

    project(0)
    for b in range(images):
        if b + 1 < images:
            project(b + 1)
        if b > 0:
            back(b - 1)
        gelu(b)
    back(images - 1)
    db_ref[...] = jnp.sum(acc_ref[...], axis=0, keepdims=True)


def weight_dots(which, cot_ref, act_ref, n_ref, gp_ref, store):
    rows = cot_ref.shape[0] * cot_ref.shape[1]

    @pl.when(which == 0)
    def _():
        store(dot(flat(cot_ref, rows), flat(act_ref, rows), 0, 0))

    @pl.when(which != 0)
    def _():
        store(dot(flat(n_ref, rows), flat(gp_ref, rows), 0, 0))


def flat(ref, rows):
    return ref[...].reshape(rows, ref.shape[2])


def send_body(cot_ref, act_ref, n_ref, gp_ref, db_ref, o_ref):
    patches = cot_ref.shape[2]
    core = lax.rem(lax.axis_index("dp"), 2)

    def store(v):
        o_ref[0:patches, :] = v.astype(BF16)

    weight_dots(1 - core, cot_ref, act_ref, n_ref, gp_ref, store)
    o_ref[patches:, :] = tiny_rows(db_ref[...])


def keep_body(cot_ref, act_ref, n_ref, gp_ref, o_ref):
    core = lax.rem(lax.axis_index("dp"), 2)

    def store(v):
        o_ref[...] = v

    weight_dots(core, cot_ref, act_ref, n_ref, gp_ref, store)


def scatter_body(radix, stride, n_got, own_ref, db_ref, *refs):
    got, (keep_ref, dbo_ref, *sends) = refs[:n_got], refs[n_got:]
    rows = own_ref.shape[0]
    chunk = rows // radix
    me = lax.rem(lax.axis_index("dp") // stride, radix)
    db = tree([join_pair(tiny_rows(db_ref[...]))] + [join_pair(g[rows:, :]) for g in got])
    dbo_ref[...] = db
    tiny = tiny_rows(db)
    for i in range(radix):
        span = slice(i * chunk, (i + 1) * chunk)
        part = own_ref[span, :]
        for g in got:
            part = part + g[span, :].astype(F32)

        @pl.when(me == i)
        def _():
            keep_ref[...] = part

        for j, send in enumerate(sends, 1):

            @pl.when(me == i ^ j)
            def _():
                send[0:chunk, :] = part.astype(BF16)

    for send in sends:
        send[chunk:, :] = tiny


def norm_body(x_ref, mr_ref, gain_ref, gn_ref, sums_ref, norm_ref, acc_ref):
    images, width, patches = x_ref.shape
    acc_ref[...] = jnp.zeros_like(acc_ref)

    def image(b, carry):
        gnf = gn_ref[b].astype(F32)
        xhat = (x_ref[b].astype(F32) - mr_ref[0, pl.ds(b, 1), :]) * mr_ref[1, pl.ds(b, 1), :]
        prod = gnf * xhat
        acc_ref[0] += prod
        acc_ref[1] += gnf
        gain = gain_ref[...]
        sums_ref[pl.ds(b, 1), :] = jnp.sum(gnf * gain, axis=0, keepdims=True)
        sums_ref[pl.ds(images + b, 1), :] = jnp.sum(prod * gain, axis=0, keepdims=True)
        return carry

    lax.fori_loop(0, images, image, 0)
    ones = jnp.ones((8, patches), F32)
    norm_ref[...] = jnp.zeros_like(norm_ref)
    for i in range(2):
        row = dot(ones, acc_ref[i], 1, 1, precision=lax.Precision.HIGHEST)
        norm_ref[0:1, i * width : (i + 1) * width] = row[0:1]


def pack_body(n_got, own_ref, db_ref, sums_ref, *refs):
    got, (o_ref,) = refs[:n_got], refs[n_got:]
    rows, hidden = own_ref.shape
    total = own_ref[...]
    for g in got:
        total = total + g[0:rows, :].astype(F32)
    o_ref[0:rows, :] = total.astype(BF16)
    db = tree([join_pair(tiny_rows(db_ref[...]))] + [join_pair(g[rows:, :]) for g in got])
    o_ref[rows : rows + EXTRA, :] = tiny_rows(db)
    n, patches = sums_ref.shape
    high, low = high_low(sums_ref[...])
    o_ref[rows + EXTRA :, :] = jnp.zeros((n, hidden), BF16)
    o_ref[rows + EXTRA :, 0:patches] = high
    o_ref[rows + EXTRA :, patches : 2 * patches] = low


def total_body(n_got, scale, channels, mine_ref, norm_ref, *refs):
    got, (o_ref, db_ref, terms_ref) = refs[:n_got], refs[n_got:]
    n, patches = terms_ref.shape
    rows = mine_ref.shape[0] - EXTRA - n
    every = (mine_ref, *got)
    o_ref[0:rows, :] = (tree([r[0:rows, :].astype(F32) for r in every]) * scale).astype(BF16)
    o_ref[rows:, :] = tiny_rows(norm_ref[...])
    db_ref[...] = tree([join_pair(r[rows : rows + EXTRA, :]) for r in every]) * scale
    sums = tree(
        [
            r[rows + EXTRA :, 0:patches].astype(F32)
            + r[rows + EXTRA :, patches : 2 * patches].astype(F32)
            for r in every
        ]
    )
    terms_ref[...] = sums / channels


def input_body(x_ref, cot_ref, gn_ref, mr_ref, gain_ref, terms_ref, o_ref):
    images = x_ref.shape[0]

    def image(b, carry):
        one = pl.ds(b, 1)
        mean, rstd = mr_ref[0, one, :], mr_ref[1, one, :]
        xhat = (x_ref[b].astype(F32) - mean) * rstd
        hat = gn_ref[b].astype(F32) * gain_ref[...]
        inner = hat - terms_ref[one, :] - xhat * terms_ref[pl.ds(images + b, 1), :]
        o_ref[b] = (cot_ref[b].astype(F32) + rstd * inner).astype(BF16)
        return carry

    lax.fori_loop(0, images, image, 0)


def gather_body(radix, stride, mine_ref, *refs):
    got, (o_ref,) = refs[:-1], refs[-1:]
    rows = mine_ref.shape[0] - EXTRA
    me = lax.rem(lax.axis_index("dp") // stride, radix)
    every = (mine_ref, *got)
    for j, r in enumerate(every):
        for i in range(radix):

            @pl.when(me == i ^ j)
            def _():
                o_ref[i * rows : (i + 1) * rows, :] = r[0:rows, :]

    o_ref[radix * rows :, :] = tiny_rows(tree([join_pair(r[rows:, :]) for r in every]))


def last_body(scale, mine_ref, got_ref, out_ref, in_ref, norm_ref):
    rows = mine_ref.shape[0] - EXTRA
    core = lax.rem(lax.axis_index("dp"), 2)
    norm_ref[...] = (join_pair(mine_ref[rows:, :]) + join_pair(got_ref[rows:, :])) * scale

    def finish(a_ref, b_ref):
        out_ref[...] = a_ref[0:rows, :].astype(F32)
        in_ref[...] = jnp.transpose(b_ref[0:rows, :].astype(F32), (1, 0))

    @pl.when(core == 0)
    def _():
        finish(mine_ref, got_ref)

    @pl.when(core != 0)
    def _():
        finish(got_ref, mine_ref)


def norm_call(x, mr, gain, gn, hidden):
    images, width, n_patch = x.shape
    return pl.pallas_call(
        norm_body,
        out_shape=[shape((2 * images, n_patch)), shape((1, hidden))],
        in_specs=[VM] * 4,
        out_specs=[VM] * 2,
        scratch_shapes=[pltpu.VMEM((2, width, n_patch), F32)],
        name="norm",
        compiler_params=LIMIT,
        cost_estimate=pl.CostEstimate(flops=1 << 29, bytes_accessed=1 << 22, transcendentals=0),
    )(x, mr, gain, gn)


def plain_plan(x, cot, mr, normed, act, gp, gn, db, gain, scale, channels):
    n_dp, n_chan = lax.axis_size("dp"), lax.axis_size("chan")
    images, width, n_patch = x.shape
    hidden = act.shape[2]
    work = 2 * images * width * n_patch * hidden
    quad = [cot, act, normed, gp]
    (send,) = call(send_body, [shape((n_patch + EXTRA, hidden), BF16)], [*quad, db], flops=work)
    radices = radices_of(n_dp)
    got = exchange_each([send], "dp", n_dp, 1)
    (own,) = call(keep_body, [shape((n_patch, hidden))], quad, flops=work)
    stride = radices[0]
    rows = n_patch
    for radix in radices[1:]:
        rows //= radix
        own, db, *sends = call(
            functools.partial(scatter_body, radix, stride, len(got)),
            [shape((rows, hidden)), shape((1, hidden))]
            + [shape((rows + EXTRA, hidden), BF16)] * (radix - 1),
            [own, db, *got],
        )
        got = exchange_each(sends, "dp", n_dp, stride)
        stride *= radix

    sums, norm = norm_call(x, mr, gain, gn, hidden)
    (message,) = call(
        functools.partial(pack_body, len(got)),
        [shape((rows + EXTRA + 2 * images, hidden), BF16)],
        [own, db, sums, *got],
    )
    others = exchange(message, "chan", n_chan, 1, n_chan)
    block, db, terms = call(
        functools.partial(total_body, len(others), 0.5 * scale, channels),
        [shape((rows + EXTRA, hidden), BF16), shape((1, hidden)), shape((2 * images, n_patch))],
        [message, norm, *others],
    )
    final = None
    for radix in radices[:0:-1]:
        stride //= radix
        got = exchange(block, "dp", n_dp, stride, radix)
        if final is None:
            (final,) = call(input_body, [shape(x.shape, BF16)], [x, cot, gn, mr, gain, terms])
        rows *= radix
        (block,) = call(
            functools.partial(gather_body, radix, stride),
            [shape((rows + EXTRA, hidden), BF16)],
            [block, *got],
        )
    (got,) = exchange(block, "dp", n_dp, 1, 2)
    dw_out, dw_in, norm = call(
        functools.partial(last_body, scale),
        [shape((n_patch, hidden)), shape((hidden, n_patch)), shape((1, hidden))],
        [block, got],
    )
    return (
        jnp.swapaxes(final, 1, 2),
        dw_in,
        dw_out,
        db[0],
        norm[0, 0:width],
        norm[0, width : 2 * width],
    )


def role_digit(radix):
    index = lax.axis_index("dp")
    return jnp.where(lax.rem(index, 2) == 0, lax.rem(index // 2, radix), lax.axis_index("chan"))


def role_pairs(n_dp, n_chan, j, swap):
    pairs = []
    for d in range(n_dp):
        for c in range(n_chan):
            e, f = (d ^ (2 * j), c) if (d % 2 == 0) != swap else (d, c ^ j)
            pairs.append((d * n_chan + c, e * n_chan + f))
    return pairs


def role_exchange(values, n_dp, n_chan, swap=False):
    got = []
    for j, v in enumerate(values, 1):
        got.append(lax.ppermute(v, ("dp", "chan"), role_pairs(n_dp, n_chan, j, swap)))
    return got


def role_send_body(cot_ref, act_ref, n_ref, gp_ref, o_ref):
    core = lax.rem(lax.axis_index("dp"), 2)

    def store(v):
        o_ref[...] = v.astype(BF16)

    weight_dots(1 - core, cot_ref, act_ref, n_ref, gp_ref, store)


def role_scatter_body(radix, own_ref, got_ref, keep_ref, *sends):
    chunk = own_ref.shape[0] // radix
    me = role_digit(radix)
    for i in range(radix):
        span = slice(i * chunk, (i + 1) * chunk)
        part = own_ref[span, :] + got_ref[span, :].astype(F32)

        @pl.when(me == i)
        def _():
            keep_ref[...] = part

        for j, send in enumerate(sends[::-1], 1):

            @pl.when(me == i ^ j)
            def _():
                send[...] = part.astype(BF16)


def role_mid_body(sums_ref, norm_ref, db_ref, o_ref):
    n, patches = sums_ref.shape
    o_ref[...] = jnp.zeros_like(o_ref)
    o_ref[0:n, 0:patches] = sums_ref[...]
    o_ref[n : n + 1, :] = norm_ref[...]
    o_ref[n + 1 : n + 2, :] = db_ref[...]


def role_pack_body(n, patches, own_ref, mid_ref, mid_got_ref, *refs):
    got, (o_ref, norm_ref) = refs[:-2], refs[-2:]
    rows, hidden = own_ref.shape
    total = own_ref[...]
    for g in got:
        total = total + g[...].astype(F32)
    o_ref[0:rows, :] = total.astype(BF16)
    side = hidden - 2 * patches
    fold = hidden // side
    db = mid_ref[n + 1 : n + 2, :] + mid_got_ref[n + 1 : n + 2, :]
    folded = [v[:, k * side : (k + 1) * side] for v in high_low(db) for k in range(fold)]
    folded.append(jnp.zeros((n - 2 * fold, side), BF16))
    o_ref[rows:, 0:patches] = mid_ref[0:n, 0:patches].astype(BF16)
    o_ref[rows:, patches : 2 * patches] = mid_got_ref[0:n, 0:patches].astype(BF16)
    o_ref[rows:, 2 * patches :] = jnp.concatenate(folded, axis=0)
    norm_ref[...] = mid_ref[n : n + 1, :] + mid_got_ref[n : n + 1, :]


def role_total_body(n, patches, scale, channels, norm_ref, *refs):
    every, (o_ref, mine_ref, other_ref) = refs[:-3], refs[-3:]
    rows = every[0].shape[0] - n
    hidden = every[0].shape[1]
    side = hidden - 2 * patches
    fold = hidden // side
    span = slice(rows, rows + n)
    o_ref[0:rows, :] = (tree([r[0:rows, :].astype(F32) for r in every]) * scale).astype(BF16)
    for k, out in enumerate((mine_ref, other_ref)):
        lanes = slice(k * patches, (k + 1) * patches)
        out[...] = tree([r[span, lanes].astype(F32) for r in every]) / channels
    folded = [r[span, 2 * patches :].astype(F32) for r in every]
    folded = tree([f[0:fold] + f[fold : 2 * fold] for f in folded])
    db = jnp.concatenate([folded[k : k + 1, :] for k in range(fold)], axis=1)
    small = [*high_low(norm_ref[...]), *high_low(db)]
    o_ref[rows:, :] = jnp.concatenate([*small, jnp.zeros((EXTRA - 4, hidden), BF16)], axis=0)


def role_input_body(
    x_ref, cot_ref, gn_ref, mr_ref, gain_ref, mine_ref, got_ref, o_ref, tick_ref, terms_ref
):
    core = lax.rem(lax.axis_index("dp"), 2)

    @pl.when(core == 0)
    def _():
        terms_ref[...] = mine_ref[...]

    @pl.when(core != 0)
    def _():
        terms_ref[...] = got_ref[...]

    input_body(x_ref, cot_ref, gn_ref, mr_ref, gain_ref, terms_ref, o_ref)
    tick_ref[...] = jnp.zeros_like(tick_ref)


def role_gather_body(radix, tick_ref, *refs):
    every, (o_ref,) = refs[:-1], refs[-1:]
    rows = every[0].shape[0] - EXTRA
    me = role_digit(radix)
    for j, r in enumerate(every):
        for i in range(radix):

            @pl.when(me == i ^ j)
            def _():
                o_ref[i * rows : (i + 1) * rows, :] = r[0:rows, :]

    small = []
    for k in (0, 2):
        total = tree(
            [r[rows + k : rows + k + 1, :].astype(F32) + r[rows + k + 1 : rows + k + 2, :].astype(F32) for r in every]
        )
        small.extend(high_low(total))
    zeros = jnp.zeros((EXTRA - 4, o_ref.shape[1]), BF16)
    o_ref[radix * rows :, :] = jnp.concatenate([*small, zeros], axis=0)


def role_last_body(scale, mine_ref, got_ref, out_ref, in_ref, db_ref, gain_ref, shift_ref):
    rows = mine_ref.shape[0] - EXTRA
    width = gain_ref.shape[0]
    core = lax.rem(lax.axis_index("dp"), 2)

    def finish(a_ref, b_ref):
        out_ref[...] = a_ref[0:rows, :].astype(F32)
        in_ref[...] = jnp.transpose(b_ref[0:rows, :].astype(F32), (1, 0))
        small = a_ref[rows : rows + 4, :].astype(F32)
        norm = (small[0:1] + small[1:2]) * scale
        db = (small[2:3] + small[3:4]) * (0.5 * scale)
        db_ref[...] = db.reshape(db_ref.shape)
        gain_ref[...] = norm[:, 0:width].reshape(gain_ref.shape)
        shift_ref[...] = norm[:, width : 2 * width].reshape(shift_ref.shape)

    @pl.when(core == 0)
    def _():
        finish(mine_ref, got_ref)

    @pl.when(core != 0)
    def _():
        finish(got_ref, mine_ref)


def role_plan(x, cot, mr, normed, act, gp, gn, db, gain, scale, channels):
    n_dp, n_chan = lax.axis_size("dp"), lax.axis_size("chan")
    images, width, n_patch = x.shape
    hidden = act.shape[2]
    n = 2 * images
    work = 2 * images * width * n_patch * hidden
    rows = n_patch // n_chan
    quad = [cot, act, normed, gp]
    pair = lambda v: exchange(v, "dp", n_dp, 1, 2)[0]

    (send,) = call(role_send_body, [shape((n_patch, hidden), BF16)], quad, work)
    got = pair(send)
    (own,) = call(keep_body, [shape((n_patch, hidden))], quad, work)
    own, *sends = call(
        functools.partial(role_scatter_body, n_chan),
        [shape((rows, hidden))] + [shape((rows, hidden), BF16)] * (n_chan - 1),
        [own, got],
    )
    got = role_exchange(sends[::-1], n_dp, n_chan)
    sums, norm = norm_call(x, mr, gain, gn, hidden)
    (mid,) = call(role_mid_body, [shape((n + 8, hidden))], [sums, norm, db])
    mid_got = pair(mid)
    message, norm = call(
        functools.partial(role_pack_body, n, n_patch),
        [shape((rows + n, hidden), BF16), shape((1, hidden))],
        [own, mid, mid_got, *got],
    )
    got = role_exchange([message] * (n_chan - 1), n_dp, n_chan, swap=True)
    block, mine, other = call(
        functools.partial(role_total_body, n, n_patch, 0.5 * scale, channels),
        [shape((rows + EXTRA, hidden), BF16), shape((n, n_patch)), shape((n, n_patch))],
        [norm, message, *got],
    )
    terms = pair(other)
    got = role_exchange([block] * (n_chan - 1), n_dp, n_chan)
    args = [x, cot, gn, mr, gain, mine, terms]
    final, tick = pl.pallas_call(
        role_input_body,
        out_shape=[shape(x.shape, BF16), shape((8, 128))],
        in_specs=[VM] * len(args),
        out_specs=[VM] * 2,
        scratch_shapes=[pltpu.VMEM((n, n_patch), F32)],
        name="input",
        compiler_params=LIMIT,
        cost_estimate=pl.CostEstimate(flops=work, bytes_accessed=1 << 22, transcendentals=0),
    )(*args)
    (block,) = call(
        functools.partial(role_gather_body, n_chan),
        [shape((n_patch + EXTRA, hidden), BF16)],
        [tick, block, *got],
    )
    outs = [shape((n_patch, hidden)), shape((hidden, n_patch)), shape((hidden,)), shape((width,)), shape((width,))]
    dw_out, dw_in, db, d_gain, d_shift = call(
        functools.partial(role_last_body, scale), outs, [block, pair(block)]
    )
    return jnp.swapaxes(final, 1, 2), dw_in, dw_out, db, d_gain, d_shift


def shards(
    patches, cotangent, w_token_in, b_token_in, w_token_out, layer_norm_gain, layer_norm_bias
):
    n_dp, n_chan = lax.axis_size("dp"), lax.axis_size("chan")
    channels = layer_norm_gain.shape[0]
    x, cot = jnp.swapaxes(patches, 1, 2), jnp.swapaxes(cotangent, 1, 2)
    images, width, n_patch = x.shape
    hidden = w_token_in.shape[0]
    scale = 1.0 / (images * n_dp)
    assert 2 * width <= hidden and 2 * n_patch <= hidden

    (sums,) = call(stats_body, [shape((2 * images, n_patch))], [x])
    others = exchange(sums, "chan", n_chan, 1, n_chan)
    gain, bias = call(
        functools.partial(spread_body, n_chan, n_patch),
        [shape((width, n_patch)), shape((width, n_patch))],
        [layer_norm_gain[None], layer_norm_bias[None]],
        flops=SPREAD,
    )
    args = [x, sums, *others, gain, bias, w_token_in, b_token_in[None], cot, w_token_out]
    outs = [
        shape((2, images, n_patch)),
        shape(x.shape, BF16),
        shape((images, width, hidden), BF16),
        shape((images, width, hidden), BF16),
        shape(x.shape, BF16),
        shape((1, hidden)),
    ]
    mr, normed, act, gp, gn, db = pl.pallas_call(
        functools.partial(main_body, n_chan, channels),
        out_shape=outs,
        in_specs=[VM] * len(args),
        out_specs=[VM] * len(outs),
        scratch_shapes=[pltpu.VMEM((width, hidden), F32)] * 4 + [pltpu.VMEM((8, hidden), F32)],
        name="main",
        compiler_params=LIMIT,
    )(*args)

    plan = role_plan if n_dp // 2 == n_chan else plain_plan
    return plan(x, cot, mr, normed, act, gp, gn, db, gain, scale, channels)


def solution(mesh):
    placed = (P("dp", None, "chan"), P("dp", None, "chan"), P(), P(), P(), P(), P())

    return jax.shard_map(
        shards,
        mesh=mesh,
        in_specs=placed,
        out_specs=(P("dp", None, "chan"), P(), P(), P(), P("chan"), P("chan")),
        check_vma=False,
    )
```

profile of v0, /device:TPU:0, one launch (start us, length us, event | category | flops | bytes accessed | tf_op | source)
XLA Modules:
  0.0 48.7 jit_solution(10259808333947500304)
XLA Ops:
  0.6 0.0 copy-start.1
  0.6 1.3 %copy-done.1 = bf16[8,256,320]{1,2,0:T(8,128)(2,1)S(1)} copy-done((bf16[8,256,320]{1,2,0:T(8,128)(2,1)S(1)}, bf16[8,256,320]{1,2,0:T(8,128)(2,1)}, u32[]{:S(2)}) %copy-start.1) | copy-done | bytes 1310744
  2.0 0.0 copy-start.5
  2.0 0.0 copy-start.6
  2.0 0.3 shard_map.118.refs_0_
  2.2 3.1 %collective-permute-start = (f32[16,256]{1,0:T(8,128)S(1)}, f32[16,256]{1,0:T(8,128)S(1)}, u32[]{:S(2)}, u32[]{:S(2)}) collective-permute-start(f32[16,256]{1,0:T(8,128)S(1)} %shard_map.118.refs_0_), channel_id=1, source_target_pairs={{0,1},{1,0},{2,3},{3,2},{4,5},{5,4},{6,7},{7,6},{8,9},{9,8},{10,11... | collective-permute-start | bytes 49160 | tf_op jit(solution)/shard_map/ppermute | solution.py:71
  5.3 2.6 %collective-permute-start.1 = (f32[16,256]{1,0:T(8,128)S(1)}, f32[16,256]{1,0:T(8,128)S(1)}, u32[]{:S(2)}, u32[]{:S(2)}) collective-permute-start(f32[16,256]{1,0:T(8,128)S(1)} %shard_map.118.refs_0_), channel_id=1, source_target_pairs={{0,2},{1,3},{2,0},{3,1},{4,6},{5,7},{6,4},{7,5},{8,10},{9,11},{10,... | collective-permute-start | bytes 49160 | tf_op jit(solution)/shard_map/ppermute | solution.py:71
  7.9 0.0 collective-permute-start.2
  7.9 0.0 copy-done.5
  7.9 0.0 copy-done.6
  8.0 0.0 copy-start.7
  8.0 0.0 copy-start
  8.0 0.0 copy-start.2
  8.0 0.0 copy-start.3
  8.0 0.0 copy-start.4
  8.0 0.2 shard_map.119
  8.2 0.4 copy-done.7
  8.7 0.0 collective-permute-done.refs_1_
  8.7 1.4 %collective-permute-done.1.refs_2_ = f32[16,256]{1,0:T(8,128)S(1)} collective-permute-done((f32[16,256]{1,0:T(8,128)S(1)}, f32[16,256]{1,0:T(8,128)S(1)}, u32[]{:S(2)}, u32[]{:S(2)}) %collective-permute-start.1) | collective-permute-done | bytes 16416 | tf_op jit(solution)/shard_map/ppermute | solution.py:71
  10.0 3.4 %collective-permute-done.2.refs_3_ = f32[16,256]{1,0:T(8,128)S(1)} collective-permute-done((f32[16,256]{1,0:T(8,128)S(1)}, f32[16,256]{1,0:T(8,128)S(1)}, u32[]{:S(2)}, u32[]{:S(2)}) %collective-permute-start.2) | collective-permute-done | bytes 16416 | tf_op jit(solution)/shard_map/ppermute | solution.py:71
  13.5 0.0 copy-done
  13.5 0.0 copy-done.2
  13.5 0.0 copy-done.3
  13.5 0.0 copy-done.4
  13.5 4.9 %main.1 = (f32[2,8,256]{2,1,0:T(8,128)S(1)}, bf16[8,320,256]{2,1,0:T(8,128)(2,1)S(1)}, bf16[8,320,640]{2,1,0:T(8,128)(2,1)S(1)}, bf16[8,320,640]{2,1,0:T(8,128)(...) custom-call(bf16[8,320,256]{2,1,0:T(8,128)(2,1)S(1)} %bitcast.8, f32[16,256]{1,0:T(8,128)S(1)} %shard_map.118.refs_0_, ...), custom_call_target="tpu_custom_call" | custom-call | tf_op jit(solution)/shard_map/main/pallas_call | solution.py:648
  18.4 1.2 %shard_map.121 = bf16[256,640]{1,0:T(8,128)(2,1)S(1)} custom-call(bf16[8,320,256]{2,1,0:T(8,128)(2,1)S(1)} %bitcast.4, bf16[8,320,640]{2,1,0:T(8,128)(2,1)S(1)} %get-tuple-element.36.act_ref, bf16[8,320,256]{2,1,0:T(8,128)(2,1)S(1)} %get-tuple-element.37.n_ref, bf16[8,320,640]{2,1,0:T(8,128)(2,1)S(1)} %get-tuple-element.38.gp_ref), custom_call_target="tpu_custom_call" | custom-call | flops 838860800 | bytes 9502720 | tf_op jit(solution)/shard_map/pallas_call | solution.py:24
  19.7 0.1 collective-permute-start.3
  19.8 1.2 %shard_map.120.own_ref = f32[256,640]{1,0:T(8,128)S(1)} custom-call(bf16[8,320,256]{2,1,0:T(8,128)(2,1)S(1)} %bitcast.5, bf16[8,320,640]{2,1,0:T(8,128)(2,1)S(1)} %get-tuple-element.36.act_ref, bf16[8,320,256]{2,1,0:T(8,128)(2,1)S(1)} %get-tuple-element.37.n_ref, bf16[8,320,640]{2,1,0:T(8,128)(2,1)S(1)} %get-tuple-element.38.gp_ref), custom_call_target="tpu_custom_call" | custom-call | flops 838860800 | bytes 9830400 | tf_op jit(solution)/shard_map/pallas_call | solution.py:24
  21.0 0.4 collective-permute-done.3.got_ref
  21.4 0.1 shard_map.122
  21.5 1.6 %collective-permute-start.5 = (bf16[64,640]{1,0:T(8,128)(2,1)S(1)}, bf16[64,640]{1,0:T(8,128)(2,1)S(1)}, u32[]{:S(2)}, u32[]{:S(2)}) collective-permute-start(bf16[64,640]{1,0:T(8,128)(2,1)S(1)} %get-tuple-element.43), channel_id=1, source_target_pairs={{0,8},{1,9},{2,10},{3,11},{4,5},{5,4},{6,7},{7,6},{8,0},{9,1},{10,... | collective-permute-start | bytes 245768 | tf_op jit(solution)/shard_map/ppermute | solution.py:425
  23.1 1.5 %collective-permute-start.6 = (bf16[64,640]{1,0:T(8,128)(2,1)S(1)}, bf16[64,640]{1,0:T(8,128)(2,1)S(1)}, u32[]{:S(2)}, u32[]{:S(2)}) collective-permute-start(bf16[64,640]{1,0:T(8,128)(2,1)S(1)} %get-tuple-element.44), channel_id=1, source_target_pairs={{0,16},{1,17},{2,18},{3,19},{4,6},{5,7},{6,4},{7,5},{8,24},{9,25},... | collective-permute-start | bytes 245768 | tf_op jit(solution)/shard_map/ppermute | solution.py:425
  24.6 0.5 collective-permute-start.7
  25.1 2.2 %norm.1 = (f32[16,256]{1,0:T(8,128)S(1)}, f32[1,640]{1,0:T(1,128)S(1)}) custom-call(bf16[8,320,256]{2,1,0:T(8,128)(2,1)S(1)} %bitcast.9, f32[2,8,256]{2,1,0:T(8,128)S(1)} %get-tuple-element.35.mr_ref, f32[320,256]{1,0:T(8,128)S(1)} %get-tuple-element.32.refs_4_.gain_ref, bf16[8,320,256]{2,1,0:T(8,128)(2,1)S(1)} %get-tuple-element.34.gn_ref), custom_call_target="tpu_custom_call" | custom-call | flops 536870912 | bytes 4194304 | tf_op jit(solution)/shard_map/norm/pallas_call | solution.py:333
  27.3 0.3 collective-permute-start.4
  27.5 1.1 %collective-permute-done.4.mid_got_ref = f32[24,640]{1,0:T(8,128)S(1)} collective-permute-done((f32[24,640]{1,0:T(8,128)S(1)}, f32[24,640]{1,0:T(8,128)S(1)}, u32[]{:S(2)}, u32[]{:S(2)}) %collective-permute-start.4) | collective-permute-done | bytes 61472 | tf_op jit(solution)/shard_map/ppermute | solution.py:71
  28.6 0.0 collective-permute-done.5.refs_0_
  28.6 0.0 collective-permute-done.6.refs_1_
  28.6 1.3 %collective-permute-done.7.refs_2_ = bf16[64,640]{1,0:T(8,128)(2,1)S(1)} collective-permute-done((bf16[64,640]{1,0:T(8,128)(2,1)S(1)}, bf16[64,640]{1,0:T(8,128)(2,1)S(1)}, u32[]{:S(2)}, u32[]{:S(2)}) %collective-permute-start.7) | collective-permute-done | bytes 81952 | tf_op jit(solution)/shard_map/ppermute | solution.py:425
  29.9 0.1 shard_map.124
  30.0 0.1 collective-permute-start.8
  30.1 0.8 %collective-permute-start.9 = (bf16[80,640]{1,0:T(8,128)(2,1)S(1)}, bf16[80,640]{1,0:T(8,128)(2,1)S(1)}, u32[]{:S(2)}, u32[]{:S(2)}) collective-permute-start(bf16[80,640]{1,0:T(8,128)(2,1)S(1)} %get-tuple-element.47.refs_0_), channel_id=1, source_target_pairs={{0,2},{1,3},{2,0},{3,1},{4,20},{5,21},{6,22},{7,23},{8,10},{9,11},... | collective-permute-start | bytes 307208 | tf_op jit(solution)/shard_map/ppermute | solution.py:425
  30.8 3.6 %collective-permute-start.10 = (bf16[80,640]{1,0:T(8,128)(2,1)S(1)}, bf16[80,640]{1,0:T(8,128)(2,1)S(1)}, u32[]{:S(2)}, u32[]{:S(2)}) collective-permute-start(bf16[80,640]{1,0:T(8,128)(2,1)S(1)} %get-tuple-element.47.refs_0_), channel_id=1, source_target_pairs={{0,3},{1,2},{2,1},{3,0},{4,28},{5,29},{6,30},{7,31},{8,11},{9,10},... | collective-permute-start | bytes 307208 | tf_op jit(solution)/shard_map/ppermute | solution.py:425
  34.4 1.4 %collective-permute-done.8.refs_1_ = bf16[80,640]{1,0:T(8,128)(2,1)S(1)} collective-permute-done((bf16[80,640]{1,0:T(8,128)(2,1)S(1)}, bf16[80,640]{1,0:T(8,128)(2,1)S(1)}, u32[]{:S(2)}, u32[]{:S(2)}) %collective-permute-start.8) | collective-permute-done | bytes 102432 | tf_op jit(solution)/shard_map/ppermute | solution.py:425
  35.8 0.0 collective-permute-done.9.refs_2_
  35.8 2.5 %collective-permute-done.10.refs_3_ = bf16[80,640]{1,0:T(8,128)(2,1)S(1)} collective-permute-done((bf16[80,640]{1,0:T(8,128)(2,1)S(1)}, bf16[80,640]{1,0:T(8,128)(2,1)S(1)}, u32[]{:S(2)}, u32[]{:S(2)}) %collective-permute-start.10) | collective-permute-done | bytes 102432 | tf_op jit(solution)/shard_map/ppermute | solution.py:425
  38.3 0.1 shard_map.125
  38.4 0.6 %collective-permute-start.12 = (bf16[80,640]{1,0:T(8,128)(2,1)S(1)}, bf16[80,640]{1,0:T(8,128)(2,1)S(1)}, u32[]{:S(2)}, u32[]{:S(2)}) collective-permute-start(bf16[80,640]{1,0:T(8,128)(2,1)S(1)} %get-tuple-element.52.refs_0_), channel_id=1, source_target_pairs={{0,8},{1,9},{2,10},{3,11},{4,5},{5,4},{6,7},{7,6},{8,0},{9,1},{10,... | collective-permute-start | bytes 307208 | tf_op jit(solution)/shard_map/ppermute | solution.py:425
  38.9 1.2 %collective-permute-start.13 = (bf16[80,640]{1,0:T(8,128)(2,1)S(1)}, bf16[80,640]{1,0:T(8,128)(2,1)S(1)}, u32[]{:S(2)}, u32[]{:S(2)}) collective-permute-start(bf16[80,640]{1,0:T(8,128)(2,1)S(1)} %get-tuple-element.52.refs_0_), channel_id=1, source_target_pairs={{0,16},{1,17},{2,18},{3,19},{4,6},{5,7},{6,4},{7,5},{8,24},{9,25},... | collective-permute-start | bytes 307208 | tf_op jit(solution)/shard_map/ppermute | solution.py:425
  40.1 1.8 %collective-permute-start.14 = (bf16[80,640]{1,0:T(8,128)(2,1)S(1)}, bf16[80,640]{1,0:T(8,128)(2,1)S(1)}, u32[]{:S(2)}, u32[]{:S(2)}) collective-permute-start(bf16[80,640]{1,0:T(8,128)(2,1)S(1)} %get-tuple-element.52.refs_0_), channel_id=1, source_target_pairs={{0,24},{1,25},{2,26},{3,27},{4,7},{5,6},{6,5},{7,4},{8,16},{9,17},... | collective-permute-start | bytes 307208 | tf_op jit(solution)/shard_map/ppermute | solution.py:425
  41.9 0.0 collective-permute-start.11
  41.9 1.2 %collective-permute-done.11.got_ref = f32[16,256]{1,0:T(8,128)S(1)} collective-permute-done((f32[16,256]{1,0:T(8,128)S(1)}, f32[16,256]{1,0:T(8,128)S(1)}, u32[]{:S(2)}, u32[]{:S(2)}) %collective-permute-start.11) | collective-permute-done | bytes 16416 | tf_op jit(solution)/shard_map/ppermute | solution.py:71
  43.1 2.1 %input.1 = (bf16[8,320,256]{2,1,0:T(8,128)(2,1)}, f32[8,128]{1,0:T(8,128)S(1)}) custom-call(bf16[8,320,256]{2,1,0:T(8,128)(2,1)S(1)} %bitcast.10, bf16[8,320,256]{2,1,0:T(8,128)(2,1)S(1)} %bitcast.6, bf16[8,320,256]{2,1,0:T(8,128)(2,1)S(1)} %get-tuple-element.34.gn_ref, f32[2,8,256]{2,1,0:T(8,128)S(1)} %get-tuple-element.35.mr_ref, ...), custom_call_target="tpu_custom_call" | custom-call | flops 838860800 | bytes 4194304 | tf_op jit(solution)/shard_map/input/pallas_call | solution.py:598
  45.2 0.0 collective-permute-done.12.refs_1_
  45.2 0.0 collective-permute-done.13.refs_2_
  45.2 0.4 collective-permute-done.14.refs_3_
  45.7 0.1 shard_map.126.mine_ref
  45.8 0.1 collective-permute-start.15
  45.8 1.6 %collective-permute-done.15.got_ref = bf16[272,640]{1,0:T(8,128)(2,1)S(1)} collective-permute-done((bf16[272,640]{1,0:T(8,128)(2,1)S(1)}, bf16[272,640]{1,0:T(8,128)(2,1)S(1)}, u32[]{:S(2)}, u32[]{:S(2)}) %collective-permute-start.15) | collective-permute-done | bytes 348192 | tf_op jit(solution)/shard_map/ppermute | solution.py:71
  47.5 1.2 %shard_map.127 = (f32[256,640]{1,0:T(8,128)}, f32[640,256]{1,0:T(8,128)}, f32[640]{0:T(1024)}, f32[320]{0:T(512)}, f32[320]{0:T(512)}) custom-call(bf16[272,640]{1,0:T(8,128)(2,1)S(1)} %shard_map.126.mine_ref, bf16[272,640]{1,0:T(8,128)(2,1)S(1)} %collective-permute-done.15.got_ref), custom_call_target="tpu_custom_call" | custom-call | bytes 2012160 | tf_op jit(solution)/shard_map/pallas_call | solution.py:24
  (4 shorter events, 0.0 us)
Async XLA Ops:
  0.6 1.3 %copy-start.1 = (bf16[8,256,320]{1,2,0:T(8,128)(2,1)S(1)}, bf16[8,256,320]{1,2,0:T(8,128)(2,1)}, u32[]{:S(2)}) copy-start(bf16[8,256,320]{1,2,0:T(8,128)(2,1)} %param.7) | copy-start | bytes 3932164
  2.0 6.0 %copy-start.5 = (f32[1280]{0:T(1024)S(1)}, f32[1280]{0:T(1024)}, u32[]{:S(2)}) copy-start(f32[1280]{0:T(1024)} %param.12) | copy-start | bytes 15364
  2.0 6.0 %copy-start.6 = (f32[1280]{0:T(1024)S(1)}, f32[1280]{0:T(1024)}, u32[]{:S(2)}) copy-start(f32[1280]{0:T(1024)} %param.13) | copy-start | bytes 15364
  2.2 6.4 %collective-permute-start = (f32[16,256]{1,0:T(8,128)S(1)}, f32[16,256]{1,0:T(8,128)S(1)}, u32[]{:S(2)}, u32[]{:S(2)}) collective-permute-start(f32[16,256]{1,0:T(8,128)S(1)} %shard_map.118.refs_0_), channel_id=1, source_target_pairs={{0,1},{1,0},{2,3},{3,2},{4,5},{5,4},{6,7},{7,6},{8,9},{9,8},{10,11... | collective-permute-start | bytes 49160 | tf_op jit(solution)/shard_map/ppermute | solution.py:71
  5.3 4.7 %collective-permute-start.1 = (f32[16,256]{1,0:T(8,128)S(1)}, f32[16,256]{1,0:T(8,128)S(1)}, u32[]{:S(2)}, u32[]{:S(2)}) collective-permute-start(f32[16,256]{1,0:T(8,128)S(1)} %shard_map.118.refs_0_), channel_id=1, source_target_pairs={{0,2},{1,3},{2,0},{3,1},{4,6},{5,7},{6,4},{7,5},{8,10},{9,11},{10,... | collective-permute-start | bytes 49160 | tf_op jit(solution)/shard_map/ppermute | solution.py:71
  7.9 5.5 %collective-permute-start.2 = (f32[16,256]{1,0:T(8,128)S(1)}, f32[16,256]{1,0:T(8,128)S(1)}, u32[]{:S(2)}, u32[]{:S(2)}) collective-permute-start(f32[16,256]{1,0:T(8,128)S(1)} %shard_map.118.refs_0_), channel_id=1, source_target_pairs={{0,3},{1,2},{2,1},{3,0},{4,7},{5,6},{6,5},{7,4},{8,11},{9,10},{10,... | collective-permute-start | bytes 49160 | tf_op jit(solution)/shard_map/ppermute | solution.py:71
  8.0 0.7 %copy-start.7 = (f32[640]{0:T(1024)S(1)}, f32[640]{0:T(1024)}, u32[]{:S(2)}) copy-start(f32[640]{0:T(1024)} %param.10) | copy-start | bytes 7684
  8.0 5.5 %copy-start = (bf16[8,256,320]{1,2,0:T(8,128)(2,1)S(1)}, bf16[8,256,320]{1,2,0:T(8,128)(2,1)}, u32[]{:S(2)}) copy-start(bf16[8,256,320]{1,2,0:T(8,128)(2,1)} %param.8) | copy-start | bytes 3932164
  8.0 5.5 %copy-start.2 = (bf16[8,256,320]{1,2,0:T(8,128)(2,1)S(1)}, bf16[8,256,320]{1,2,0:T(8,128)(2,1)}, u32[]{:S(2)}) copy-start(bf16[8,256,320]{1,2,0:T(8,128)(2,1)} %param.7) | copy-start | bytes 3932164
  8.0 5.5 %copy-start.3 = (bf16[640,256]{1,0:T(8,128)(2,1)S(1)}, bf16[640,256]{1,0:T(8,128)(2,1)}, u32[]{:S(2)}) copy-start(bf16[640,256]{1,0:T(8,128)(2,1)} %refs_6_.1) | copy-start | bytes 983044
  8.0 5.5 %copy-start.4 = (bf16[256,640]{1,0:T(8,128)(2,1)S(1)}, bf16[256,640]{1,0:T(8,128)(2,1)}, u32[]{:S(2)}) copy-start(bf16[256,640]{1,0:T(8,128)(2,1)} %refs_9_.1) | copy-start | bytes 983044
  19.7 1.7 %collective-permute-start.3 = (bf16[256,640]{1,0:T(8,128)(2,1)S(1)}, bf16[256,640]{1,0:T(8,128)(2,1)S(1)}, u32[]{:S(2)}, u32[]{:S(2)}) collective-permute-start(bf16[256,640]{1,0:T(8,128)(2,1)S(1)} %shard_map.121), channel_id=1, source_target_pairs={{0,4},{4,0},{8,12},{12,8},{16,20},{20,16},{24,28},{28,24},{1,5},{5... | collective-permute-start | bytes 983048 | tf_op jit(solution)/shard_map/ppermute | solution.py:71
  21.5 7.1 %collective-permute-start.5 = (bf16[64,640]{1,0:T(8,128)(2,1)S(1)}, bf16[64,640]{1,0:T(8,128)(2,1)S(1)}, u32[]{:S(2)}, u32[]{:S(2)}) collective-permute-start(bf16[64,640]{1,0:T(8,128)(2,1)S(1)} %get-tuple-element.43), channel_id=1, source_target_pairs={{0,8},{1,9},{2,10},{3,11},{4,5},{5,4},{6,7},{7,6},{8,0},{9,1},{10,... | collective-permute-start | bytes 245768 | tf_op jit(solution)/shard_map/ppermute | solution.py:425
  23.1 5.5 %collective-permute-start.6 = (bf16[64,640]{1,0:T(8,128)(2,1)S(1)}, bf16[64,640]{1,0:T(8,128)(2,1)S(1)}, u32[]{:S(2)}, u32[]{:S(2)}) collective-permute-start(bf16[64,640]{1,0:T(8,128)(2,1)S(1)} %get-tuple-element.44), channel_id=1, source_target_pairs={{0,16},{1,17},{2,18},{3,19},{4,6},{5,7},{6,4},{7,5},{8,24},{9,25},... | collective-permute-start | bytes 245768 | tf_op jit(solution)/shard_map/ppermute | solution.py:425
  24.6 5.3 %collective-permute-start.7 = (bf16[64,640]{1,0:T(8,128)(2,1)S(1)}, bf16[64,640]{1,0:T(8,128)(2,1)S(1)}, u32[]{:S(2)}, u32[]{:S(2)}) collective-permute-start(bf16[64,640]{1,0:T(8,128)(2,1)S(1)} %get-tuple-element.45), channel_id=1, source_target_pairs={{0,24},{1,25},{2,26},{3,27},{4,7},{5,6},{6,5},{7,4},{8,16},{9,17},... | collective-permute-start | bytes 245768 | tf_op jit(solution)/shard_map/ppermute | solution.py:425
  27.3 1.3 %collective-permute-start.4 = (f32[24,640]{1,0:T(8,128)S(1)}, f32[24,640]{1,0:T(8,128)S(1)}, u32[]{:S(2)}, u32[]{:S(2)}) collective-permute-start(f32[24,640]{1,0:T(8,128)S(1)} %shard_map.123.mid_ref), channel_id=1, source_target_pairs={{0,4},{4,0},{8,12},{12,8},{16,20},{20,16},{24,28},{28,24},{1,5},{5... | collective-permute-start | bytes 184328 | tf_op jit(solution)/shard_map/ppermute | solution.py:71
  30.0 5.8 %collective-permute-start.8 = (bf16[80,640]{1,0:T(8,128)(2,1)S(1)}, bf16[80,640]{1,0:T(8,128)(2,1)S(1)}, u32[]{:S(2)}, u32[]{:S(2)}) collective-permute-start(bf16[80,640]{1,0:T(8,128)(2,1)S(1)} %get-tuple-element.47.refs_0_), channel_id=1, source_target_pairs={{0,1},{1,0},{2,3},{3,2},{4,12},{5,13},{6,14},{7,15},{8,9},{9,8},{1... | collective-permute-start | bytes 307208 | tf_op jit(solution)/shard_map/ppermute | solution.py:425
  30.1 5.7 %collective-permute-start.9 = (bf16[80,640]{1,0:T(8,128)(2,1)S(1)}, bf16[80,640]{1,0:T(8,128)(2,1)S(1)}, u32[]{:S(2)}, u32[]{:S(2)}) collective-permute-start(bf16[80,640]{1,0:T(8,128)(2,1)S(1)} %get-tuple-element.47.refs_0_), channel_id=1, source_target_pairs={{0,2},{1,3},{2,0},{3,1},{4,20},{5,21},{6,22},{7,23},{8,10},{9,11},... | collective-permute-start | bytes 307208 | tf_op jit(solution)/shard_map/ppermute | solution.py:425
  30.8 7.5 %collective-permute-start.10 = (bf16[80,640]{1,0:T(8,128)(2,1)S(1)}, bf16[80,640]{1,0:T(8,128)(2,1)S(1)}, u32[]{:S(2)}, u32[]{:S(2)}) collective-permute-start(bf16[80,640]{1,0:T(8,128)(2,1)S(1)} %get-tuple-element.47.refs_0_), channel_id=1, source_target_pairs={{0,3},{1,2},{2,1},{3,0},{4,28},{5,29},{6,30},{7,31},{8,11},{9,10},... | collective-permute-start | bytes 307208 | tf_op jit(solution)/shard_map/ppermute | solution.py:425
  38.4 6.9 %collective-permute-start.12 = (bf16[80,640]{1,0:T(8,128)(2,1)S(1)}, bf16[80,640]{1,0:T(8,128)(2,1)S(1)}, u32[]{:S(2)}, u32[]{:S(2)}) collective-permute-start(bf16[80,640]{1,0:T(8,128)(2,1)S(1)} %get-tuple-element.52.refs_0_), channel_id=1, source_target_pairs={{0,8},{1,9},{2,10},{3,11},{4,5},{5,4},{6,7},{7,6},{8,0},{9,1},{10,... | collective-permute-start | bytes 307208 | tf_op jit(solution)/shard_map/ppermute | solution.py:425
  38.9 6.3 %collective-permute-start.13 = (bf16[80,640]{1,0:T(8,128)(2,1)S(1)}, bf16[80,640]{1,0:T(8,128)(2,1)S(1)}, u32[]{:S(2)}, u32[]{:S(2)}) collective-permute-start(bf16[80,640]{1,0:T(8,128)(2,1)S(1)} %get-tuple-element.52.refs_0_), channel_id=1, source_target_pairs={{0,16},{1,17},{2,18},{3,19},{4,6},{5,7},{6,4},{7,5},{8,24},{9,25},... | collective-permute-start | bytes 307208 | tf_op jit(solution)/shard_map/ppermute | solution.py:425
  40.1 5.6 %collective-permute-start.14 = (bf16[80,640]{1,0:T(8,128)(2,1)S(1)}, bf16[80,640]{1,0:T(8,128)(2,1)S(1)}, u32[]{:S(2)}, u32[]{:S(2)}) collective-permute-start(bf16[80,640]{1,0:T(8,128)(2,1)S(1)} %get-tuple-element.52.refs_0_), channel_id=1, source_target_pairs={{0,24},{1,25},{2,26},{3,27},{4,7},{5,6},{6,5},{7,4},{8,16},{9,17},... | collective-permute-start | bytes 307208 | tf_op jit(solution)/shard_map/ppermute | solution.py:425
  41.9 1.2 %collective-permute-start.11 = (f32[16,256]{1,0:T(8,128)S(1)}, f32[16,256]{1,0:T(8,128)S(1)}, u32[]{:S(2)}, u32[]{:S(2)}) collective-permute-start(f32[16,256]{1,0:T(8,128)S(1)} %get-tuple-element.49), channel_id=1, source_target_pairs={{0,4},{4,0},{8,12},{12,8},{16,20},{20,16},{24,28},{28,24},{1,5},{5... | collective-permute-start | bytes 49160 | tf_op jit(solution)/shard_map/ppermute | solution.py:71
  45.8 1.7 %collective-permute-start.15 = (bf16[272,640]{1,0:T(8,128)(2,1)S(1)}, bf16[272,640]{1,0:T(8,128)(2,1)S(1)}, u32[]{:S(2)}, u32[]{:S(2)}) collective-permute-start(bf16[272,640]{1,0:T(8,128)(2,1)S(1)} %shard_map.126.mine_ref), channel_id=1, source_target_pairs={{0,4},{4,0},{8,12},{12,8},{16,20},{20,16},{24,28},{28,24},{1,5},{5... | collective-permute-start | bytes 1044488 | tf_op jit(solution)/shard_map/ppermute | solution.py:71
where the time goes:
time: 48.9 us; the launch traced here: 48.7 us
  starting transfers between devices  17.7 us (36%)
  waiting for transfers between devices  14.7 us (30%)
  Pallas kernels  13.8 us (28%)
  local copies, waits for them, and re-layouts  1.8 us (4%)
  between operations  0.8 us (2%)
    ppermute x9, starting transfers between devices, role_exchange(): lax.ppermute(v, ('dp', 'chan'), role_pairs(n_dp, n_chan, j, swap))  11.6 us
    ppermute x7, waiting for transfers between devices, exchange(): lax.ppermute(value, axis, [(i, i ^ j * stride) for i in range(n)])  9.06 us
    ppermute x7, starting transfers between devices, exchange(): lax.ppermute(value, axis, [(i, i ^ j * stride) for i in range(n)])  6.11 us
    ppermute x9, waiting for transfers between devices, role_exchange(): lax.ppermute(v, ('dp', 'chan'), role_pairs(n_dp, n_chan, j, swap))  5.63 us
    pallas_call x1, Pallas kernels, shards(): pl.pallas_call(functools.partial(main_body, n_chan, channels), out_shape=...  4.94 us
    pallas_call x10, Pallas kernels, call(): pl.pallas_call(body, out_shape=outs, in_specs=[VM] * len(args), out_specs...  4.51 us
    pallas_call x1, Pallas kernels, norm_call(): pl.pallas_call(norm_body, out_shape=[shape((2 * images, n_patch)), shape(...  2.21 us
    pallas_call x1, Pallas kernels, role_plan(): pl.pallas_call(role_input_body, out_shape=[shape(x.shape, BF16), shape((8...  2.13 us
  transfers between devices with their start and end apart: 16, of which 10 were waited for; matrix products, arithmetic and copies ran while one was open for 0% of the time, Pallas kernels for 12%

commit v1 on v0

--- a/solution.py
+++ b/solution.py
@@ -16,6 +16,7 @@
 F32 = jnp.float32
 BF16 = jnp.bfloat16
 VM = pl.BlockSpec(memory_space=pltpu.VMEM)
+HB = pl.BlockSpec(memory_space=pltpu.HBM)
 LIMIT = pltpu.CompilerParams(vmem_limit_bytes=24 << 20)
 
 
@@ -112,15 +113,15 @@
 def main_body(n_parts, channels, x_ref, *refs):
     parts = refs[:n_parts]
     gain_ref, bias_ref, w_ref, b_ref, cot_ref, w_out_ref = refs[n_parts : n_parts + 6]
-    mr_ref, n_ref, act_ref, gp_ref, gn_ref, db_ref, *work_refs, acc_ref = refs[n_parts + 6 :]
+    mr_ref, n_ref, act_ref, gp_ref, send_ref, *work_refs, acc_ref = refs[n_parts + 6 :]
     pre_refs, ga_refs = work_refs[:2], work_refs[2:]
-    images, width, _ = x_ref.shape
+    images, width, patches = x_ref.shape
     totals = tree([p[...] for p in parts]) / channels
     mean = totals[:images]
     rstd = lax.rsqrt(totals[images:] - mean * mean + eps_norm)
     mr_ref[0] = mean
     mr_ref[1] = rstd
-    acc_ref[...] = jnp.zeros_like(acc_ref)
+    core = lax.rem(lax.axis_index("dp"), 2)
     step = STEP
 
     def project(b):
@@ -130,8 +131,12 @@
         pre_refs[b % 2][...] = dot(normed, w_ref[...], 1, 1)
         ga_refs[b % 2][...] = dot(cot_ref[b], w_out_ref[...], 1, 0)
 
-    def back(b):
-        gn_ref[b] = (0.5 * dot(gp_ref[b], w_ref[...], 1, 0)).astype(BF16)
+    def partner_grad(b):
+        pair, rows = slice(b, b + 2), 2 * width
+        left = jnp.where(core == 0, n_ref[pair], cot_ref[pair]).reshape(rows, patches)
+        right = jnp.where(core == 0, gp_ref[pair], act_ref[pair]).reshape(rows, gp_ref.shape[2])
+        part = dot(left, right, 0, 0)
+        acc_ref[...] = part if b == 0 else acc_ref[...] + part
 
     def gelu(b):
         for r in range(0, width, step):
@@ -141,22 +146,17 @@
             act_ref[b, rows, :] = (pre * twice).astype(BF16)
             bell = jnp.exp2((pre * pre) * (-0.5 / math.log(2.0)))
             slope = twice + (pre * math.sqrt(2.0 / math.pi)) * bell
-            gp = (ga_refs[b % 2][rows, :] * slope).astype(BF16)
-            gp_ref[b, rows, :] = gp
-            gpf = gp.astype(F32)
-            acc_ref[...] += functools.reduce(
-                jnp.add, [gpf[i : i + 8] for i in range(0, step, 8)]
-            )
+            gp_ref[b, rows, :] = (ga_refs[b % 2][rows, :] * slope).astype(BF16)
 
     project(0)
     for b in range(images):
         if b + 1 < images:
             project(b + 1)
-        if b > 0:
-            back(b - 1)
+        if b > 0 and b % 2 == 0:
+            partner_grad(b - 2)
         gelu(b)
-    back(images - 1)
-    db_ref[...] = jnp.sum(acc_ref[...], axis=0, keepdims=True)
+    partner_grad(images - 2)
+    send_ref[...] = acc_ref[...].astype(BF16)
 
 
 def weight_dots(which, cot_ref, act_ref, n_ref, gp_ref, store):
@@ -223,19 +223,53 @@
         send[chunk:, :] = tiny
 
 
-def norm_body(x_ref, mr_ref, gain_ref, gn_ref, sums_ref, norm_ref, acc_ref):
+def back_body(x_ref, mr_ref, gain_ref, gp_ref, w_ref, gn_ref, sums_ref, db_ref, acc_ref):
+    images, width = x_ref.shape[0], x_ref.shape[1]
+
+    def project(b):
+        gn_ref[b] = (0.5 * dot(gp_ref[b], w_ref[...], 1, 0)).astype(BF16)
+
+    def reduce(b):
+        xhat = (x_ref[b].astype(F32) - mr_ref[0, b : b + 1, :]) * mr_ref[1, b : b + 1, :]
+        hat = gn_ref[b].astype(F32) * gain_ref[...]
+        sums_ref[b : b + 1, :] = jnp.sum(hat, axis=0, keepdims=True)
+        sums_ref[images + b : images + b + 1, :] = jnp.sum(hat * xhat, axis=0, keepdims=True)
+        gp = gp_ref[b].astype(F32)
+        part = functools.reduce(jnp.add, [gp[i : i + 8] for i in range(0, width, 8)])
+        acc_ref[...] = part if b == 0 else acc_ref[...] + part
+
+    project(0)
+    for b in range(images):
+        if b + 1 < images:
+            project(b + 1)
+        reduce(b)
+    db_ref[...] = jnp.sum(acc_ref[...], axis=0, keepdims=True)
+
+
+def back_call(x, mr, gain, gp, w_token_in):
+    images, _, n_patch = x.shape
+    hidden = gp.shape[2]
+    return pl.pallas_call(
+        back_body,
+        out_shape=[shape(x.shape, BF16), shape((2 * images, n_patch)), shape((1, hidden))],
+        in_specs=[VM] * 5,
+        out_specs=[VM] * 3,
+        scratch_shapes=[pltpu.VMEM((8, hidden), F32)],
+        name="back",
+        compiler_params=LIMIT,
+        cost_estimate=pl.CostEstimate(flops=1 << 30, bytes_accessed=1 << 22, transcendentals=0),
+    )(x, mr, gain, gp, w_token_in)
+
+
+def norm_body(x_ref, mr_ref, gn_ref, norm_ref, acc_ref):
     images, width, patches = x_ref.shape
     acc_ref[...] = jnp.zeros_like(acc_ref)
 
     def image(b, carry):
         gnf = gn_ref[b].astype(F32)
         xhat = (x_ref[b].astype(F32) - mr_ref[0, pl.ds(b, 1), :]) * mr_ref[1, pl.ds(b, 1), :]
-        prod = gnf * xhat
-        acc_ref[0] += prod
+        acc_ref[0] += gnf * xhat
         acc_ref[1] += gnf
-        gain = gain_ref[...]
-        sums_ref[pl.ds(b, 1), :] = jnp.sum(gnf * gain, axis=0, keepdims=True)
-        sums_ref[pl.ds(images + b, 1), :] = jnp.sum(prod * gain, axis=0, keepdims=True)
         return carry
 
     lax.fori_loop(0, images, image, 0)
@@ -328,25 +362,26 @@
         finish(got_ref, mine_ref)
 
 
-def norm_call(x, mr, gain, gn, hidden):
-    images, width, n_patch = x.shape
+def norm_call(x, mr, gn, hidden):
+    _, width, n_patch = x.shape
     return pl.pallas_call(
         norm_body,
-        out_shape=[shape((2 * images, n_patch)), shape((1, hidden))],
-        in_specs=[VM] * 4,
-        out_specs=[VM] * 2,
+        out_shape=shape((1, hidden)),
+        in_specs=[VM] * 3,
+        out_specs=VM,
         scratch_shapes=[pltpu.VMEM((2, width, n_patch), F32)],
         name="norm",
         compiler_params=LIMIT,
         cost_estimate=pl.CostEstimate(flops=1 << 29, bytes_accessed=1 << 22, transcendentals=0),
-    )(x, mr, gain, gn)
-
-
-def plain_plan(x, cot, mr, normed, act, gp, gn, db, gain, scale, channels):
+    )(x, mr, gn)
+
+
+def plain_plan(x, cot, mr, normed, act, gp, send, gain, w_token_in, scale, channels):
     n_dp, n_chan = lax.axis_size("dp"), lax.axis_size("chan")
     images, width, n_patch = x.shape
     hidden = act.shape[2]
     work = 2 * images * width * n_patch * hidden
+    gn, sums, db = back_call(x, mr, gain, gp, w_token_in)
     quad = [cot, act, normed, gp]
     (send,) = call(send_body, [shape((n_patch + EXTRA, hidden), BF16)], [*quad, db], flops=work)
     radices = radices_of(n_dp)
@@ -365,7 +400,7 @@
         got = exchange_each(sends, "dp", n_dp, stride)
         stride *= radix
 
-    sums, norm = norm_call(x, mr, gain, gn, hidden)
+    norm = norm_call(x, mr, gn, hidden)
     (message,) = call(
         functools.partial(pack_body, len(got)),
         [shape((rows + EXTRA + 2 * images, hidden), BF16)],
@@ -421,18 +456,9 @@
 
 def role_exchange(values, n_dp, n_chan, swap=False):
     got = []
-    for j, v in enumerate(values, 1):
+    for j, v in reversed(list(enumerate(values, 1))):
         got.append(lax.ppermute(v, ("dp", "chan"), role_pairs(n_dp, n_chan, j, swap)))
-    return got
-
-
-def role_send_body(cot_ref, act_ref, n_ref, gp_ref, o_ref):
-    core = lax.rem(lax.axis_index("dp"), 2)
-
-    def store(v):
-        o_ref[...] = v.astype(BF16)
-
-    weight_dots(1 - core, cot_ref, act_ref, n_ref, gp_ref, store)
+    return got[::-1]
 
 
 def role_scatter_body(radix, own_ref, got_ref, keep_ref, *sends):
@@ -453,123 +479,139 @@
                 send[...] = part.astype(BF16)
 
 
-def role_mid_body(sums_ref, norm_ref, db_ref, o_ref):
-    n, patches = sums_ref.shape
-    o_ref[...] = jnp.zeros_like(o_ref)
-    o_ref[0:n, 0:patches] = sums_ref[...]
-    o_ref[n : n + 1, :] = norm_ref[...]
-    o_ref[n + 1 : n + 2, :] = db_ref[...]
-
-
-def role_pack_body(n, patches, own_ref, mid_ref, mid_got_ref, *refs):
-    got, (o_ref, norm_ref) = refs[:-2], refs[-2:]
+def side_block(sums, db, hidden):
+    images, patches = sums.shape[0] // 2, sums.shape[1]
+    side = hidden - 2 * patches
+    folded = [db[:, k : k + side] for k in range(0, hidden, side)]
+    folded.append(jnp.zeros((images - len(folded), side), F32))
+    parts = [sums[:images], sums[images:], jnp.concatenate(folded, axis=0)]
+    return jnp.concatenate(parts, axis=1).astype(BF16)
+
+
+def side_db(block, patches):
+    side = block.shape[1] - 2 * patches
+    fold = block.shape[1] // side
+    return jnp.concatenate([block[k : k + 1, 2 * patches :] for k in range(fold)], axis=1)
+
+
+def side_fits(images, patches, hidden):
+    side = hidden - 2 * patches
+    return side > 0 and side % 128 == 0 and hidden % side == 0 and max(4, hidden // side) <= images
+
+
+def role_pack_body(own_ref, sums_ref, db_ref, *refs):
+    got, (o_ref,) = refs[:-1], refs[-1:]
     rows, hidden = own_ref.shape
     total = own_ref[...]
     for g in got:
         total = total + g[...].astype(F32)
     o_ref[0:rows, :] = total.astype(BF16)
-    side = hidden - 2 * patches
-    fold = hidden // side
-    db = mid_ref[n + 1 : n + 2, :] + mid_got_ref[n + 1 : n + 2, :]
-    folded = [v[:, k * side : (k + 1) * side] for v in high_low(db) for k in range(fold)]
-    folded.append(jnp.zeros((n - 2 * fold, side), BF16))
-    o_ref[rows:, 0:patches] = mid_ref[0:n, 0:patches].astype(BF16)
-    o_ref[rows:, patches : 2 * patches] = mid_got_ref[0:n, 0:patches].astype(BF16)
-    o_ref[rows:, 2 * patches :] = jnp.concatenate(folded, axis=0)
-    norm_ref[...] = mid_ref[n : n + 1, :] + mid_got_ref[n : n + 1, :]
-
-
-def role_total_body(n, patches, scale, channels, norm_ref, *refs):
-    every, (o_ref, mine_ref, other_ref) = refs[:-3], refs[-3:]
-    rows = every[0].shape[0] - n
-    hidden = every[0].shape[1]
-    side = hidden - 2 * patches
-    fold = hidden // side
-    span = slice(rows, rows + n)
+    o_ref[rows:, :] = side_block(sums_ref[...], db_ref[...], hidden)
+
+
+def role_total_body(scale, norm_ref, norm_got_ref, sums_ref, *refs):
+    every, (o_ref,) = refs[:-1], refs[-1:]
+    images, patches = sums_ref.shape[0] // 2, sums_ref.shape[1]
+    rows, hidden = o_ref.shape[0] - images, o_ref.shape[1]
+    core = lax.rem(lax.axis_index("dp"), 2)
     o_ref[0:rows, :] = (tree([r[0:rows, :].astype(F32) for r in every]) * scale).astype(BF16)
-    for k, out in enumerate((mine_ref, other_ref)):
-        lanes = slice(k * patches, (k + 1) * patches)
-        out[...] = tree([r[span, lanes].astype(F32) for r in every]) / channels
-    folded = [r[span, 2 * patches :].astype(F32) for r in every]
-    folded = tree([f[0:fold] + f[fold : 2 * fold] for f in folded])
-    db = jnp.concatenate([folded[k : k + 1, :] for k in range(fold)], axis=1)
-    small = [*high_low(norm_ref[...]), *high_low(db)]
-    o_ref[rows:, :] = jnp.concatenate([*small, jnp.zeros((EXTRA - 4, hidden), BF16)], axis=0)
-
-
-def role_input_body(
-    x_ref, cot_ref, gn_ref, mr_ref, gain_ref, mine_ref, got_ref, o_ref, tick_ref, terms_ref
-):
+    db = side_db(tree([r[rows:, :].astype(F32) for r in every]), patches)
+
+    @pl.when(core == 0)
+    def _():
+        small = [*high_low(norm_ref[...] + norm_got_ref[...]), *high_low(db)]
+        small.append(jnp.zeros((images - 4, hidden), BF16))
+        o_ref[rows:, :] = jnp.concatenate(small, axis=0)
+
+    @pl.when(core != 0)
+    def _():
+        o_ref[rows:, :] = side_block(sums_ref[...], db, hidden)
+
+
+def role_input_body(radix, channels, x_ref, cot_ref, gn_ref, mr_ref, gain_ref, *refs):
+    even, odd = refs[:radix], refs[radix : 2 * radix]
+    o_hbm, terms_ref, o_ref, sems = refs[2 * radix :]
+    images, patches = x_ref.shape[0], x_ref.shape[2]
+    rows = even[0].shape[0] - images
     core = lax.rem(lax.axis_index("dp"), 2)
 
+    def terms(every):
+        for k in range(2):
+            lanes = slice(k * patches, (k + 1) * patches)
+            total = tree([r[rows:, lanes].astype(F32) for r in every])
+            terms_ref[k * images : (k + 1) * images, :] = total / channels
+
     @pl.when(core == 0)
     def _():
-        terms_ref[...] = mine_ref[...]
+        terms(even)
 
     @pl.when(core != 0)
     def _():
-        terms_ref[...] = got_ref[...]
-
-    input_body(x_ref, cot_ref, gn_ref, mr_ref, gain_ref, terms_ref, o_ref)
-    tick_ref[...] = jnp.zeros_like(tick_ref)
-
-
-def role_gather_body(radix, tick_ref, *refs):
-    every, (o_ref,) = refs[:-1], refs[-1:]
-    rows = every[0].shape[0] - EXTRA
-    me = role_digit(radix)
-    for j, r in enumerate(every):
+        terms(odd)
+
+    copies = []
+    for b in range(images):
+        mean, rstd = mr_ref[0, b : b + 1, :], mr_ref[1, b : b + 1, :]
+        xhat = (x_ref[b].astype(F32) - mean) * rstd
+        hat = gn_ref[b].astype(F32) * gain_ref[...]
+        inner = hat - terms_ref[b : b + 1, :] - xhat * terms_ref[images + b : images + b + 1, :]
+        o_ref[b] = (cot_ref[b].astype(F32) + rstd * inner).astype(BF16)
+        copy = pltpu.make_async_copy(o_ref.at[b], o_hbm.at[b], sems.at[b])
+        copy.start()
+        copies.append(copy)
+    for copy in copies:
+        copy.wait()
+
+
+def role_last_body(radix, scale, *refs):
+    mine, got = refs[:radix], refs[radix : 2 * radix]
+    out_ref, in_ref, db_ref, gain_ref, shift_ref, held_ref = refs[2 * radix :]
+    width = gain_ref.shape[0]
+    patches, _ = out_ref.shape
+    rows = patches // radix
+    core = lax.rem(lax.axis_index("dp"), 2)
+    first = lax.rem(lax.axis_index("dp") // 2, radix)
+    second = lax.axis_index("chan")
+
+    def place(dst, digit, j, ref):
         for i in range(radix):
 
-            @pl.when(me == i ^ j)
+            @pl.when(digit == i ^ j)
             def _():
-                o_ref[i * rows : (i + 1) * rows, :] = r[0:rows, :]
-
-    small = []
-    for k in (0, 2):
-        total = tree(
-            [r[rows + k : rows + k + 1, :].astype(F32) + r[rows + k + 1 : rows + k + 2, :].astype(F32) for r in every]
-        )
-        small.extend(high_low(total))
-    zeros = jnp.zeros((EXTRA - 4, o_ref.shape[1]), BF16)
-    o_ref[radix * rows :, :] = jnp.concatenate([*small, zeros], axis=0)
-
-
-def role_last_body(scale, mine_ref, got_ref, out_ref, in_ref, db_ref, gain_ref, shift_ref):
-    rows = mine_ref.shape[0] - EXTRA
-    width = gain_ref.shape[0]
-    core = lax.rem(lax.axis_index("dp"), 2)
-
-    def finish(a_ref, b_ref):
-        out_ref[...] = a_ref[0:rows, :].astype(F32)
-        in_ref[...] = jnp.transpose(b_ref[0:rows, :].astype(F32), (1, 0))
-        small = a_ref[rows : rows + 4, :].astype(F32)
+                dst[i * rows : (i + 1) * rows, :] = ref[0:rows, :].astype(dst.dtype)
+
+    def finish(outs, ins):
+        for j in range(radix):
+            place(out_ref, first, j, outs[j])
+            place(held_ref, second, j, ins[j])
+        small = tree([r[rows : rows + 4, :].astype(F32) for r in outs])
         norm = (small[0:1] + small[1:2]) * scale
-        db = (small[2:3] + small[3:4]) * (0.5 * scale)
+        db = small[2:3] + small[3:4] + side_db(tree([r[rows:, :].astype(F32) for r in ins]), patches)
+        db = db * (0.5 * scale)
         db_ref[...] = db.reshape(db_ref.shape)
         gain_ref[...] = norm[:, 0:width].reshape(gain_ref.shape)
         shift_ref[...] = norm[:, width : 2 * width].reshape(shift_ref.shape)
 
     @pl.when(core == 0)
     def _():
-        finish(mine_ref, got_ref)
+        finish(mine, got)
 
     @pl.when(core != 0)
     def _():
-        finish(got_ref, mine_ref)
-
-
-def role_plan(x, cot, mr, normed, act, gp, gn, db, gain, scale, channels):
+        finish(got, mine)
+
+    in_ref[...] = jnp.transpose(held_ref[...].astype(F32), (1, 0))
+
+
+def role_plan(x, cot, mr, normed, act, gp, send, gain, w_token_in, scale, channels):
     n_dp, n_chan = lax.axis_size("dp"), lax.axis_size("chan")
     images, width, n_patch = x.shape
     hidden = act.shape[2]
-    n = 2 * images
     work = 2 * images * width * n_patch * hidden
     rows = n_patch // n_chan
     quad = [cot, act, normed, gp]
     pair = lambda v: exchange(v, "dp", n_dp, 1, 2)[0]
 
-    (send,) = call(role_send_body, [shape((n_patch, hidden), BF16)], quad, work)
     got = pair(send)
     (own,) = call(keep_body, [shape((n_patch, hidden))], quad, work)
     own, *sends = call(
@@ -578,42 +620,55 @@
         [own, got],
     )
     got = role_exchange(sends[::-1], n_dp, n_chan)
-    sums, norm = norm_call(x, mr, gain, gn, hidden)
-    (mid,) = call(role_mid_body, [shape((n + 8, hidden))], [sums, norm, db])
-    mid_got = pair(mid)
-    message, norm = call(
-        functools.partial(role_pack_body, n, n_patch),
-        [shape((rows + n, hidden), BF16), shape((1, hidden))],
-        [own, mid, mid_got, *got],
-    )
+    gn, sums, db = back_call(x, mr, gain, gp, w_token_in)
+    (message,) = call(role_pack_body, [shape((rows + images, hidden), BF16)], [own, sums, db, *got])
     got = role_exchange([message] * (n_chan - 1), n_dp, n_chan, swap=True)
-    block, mine, other = call(
-        functools.partial(role_total_body, n, n_patch, 0.5 * scale, channels),
-        [shape((rows + EXTRA, hidden), BF16), shape((n, n_patch)), shape((n, n_patch))],
-        [norm, message, *got],
-    )
-    terms = pair(other)
+    norm = norm_call(x, mr, gn, hidden)
+    norm_got = pair(norm)
+    messages = [message, *got]
+    (block,) = call(
+        functools.partial(role_total_body, 0.5 * scale),
+        [shape((rows + images, hidden), BF16)],
+        [norm, norm_got, sums, *messages],
+    )
     got = role_exchange([block] * (n_chan - 1), n_dp, n_chan)
-    args = [x, cot, gn, mr, gain, mine, terms]
-    final, tick = pl.pallas_call(
-        role_input_body,
-        out_shape=[shape(x.shape, BF16), shape((8, 128))],
+    every = [block, *got]
+    args = [x, cot, gn, mr, gain, *messages, *every]
+    final = pl.pallas_call(
+        functools.partial(role_input_body, n_chan, channels),
+        out_shape=shape(x.shape, BF16),
         in_specs=[VM] * len(args),
-        out_specs=[VM] * 2,
-        scratch_shapes=[pltpu.VMEM((n, n_patch), F32)],
+        out_specs=HB,
+        scratch_shapes=[
+            pltpu.VMEM((2 * images, n_patch), F32),
+            pltpu.VMEM(x.shape, BF16),
+            pltpu.SemaphoreType.DMA((images,)),
+        ],
         name="input",
         compiler_params=LIMIT,
         cost_estimate=pl.CostEstimate(flops=work, bytes_accessed=1 << 22, transcendentals=0),
     )(*args)
-    (block,) = call(
-        functools.partial(role_gather_body, n_chan),
-        [shape((n_patch + EXTRA, hidden), BF16)],
-        [tick, block, *got],
-    )
-    outs = [shape((n_patch, hidden)), shape((hidden, n_patch)), shape((hidden,)), shape((width,)), shape((width,))]
-    dw_out, dw_in, db, d_gain, d_shift = call(
-        functools.partial(role_last_body, scale), outs, [block, pair(block)]
-    )
+    onward = {}
+    for j in (0, *range(n_chan - 1, 0, -1)):
+        onward[j] = pair(every[j])
+    args = [*every, *(onward[j] for j in range(n_chan))]
+    dw_out, dw_in, db, d_gain, d_shift = pl.pallas_call(
+        functools.partial(role_last_body, n_chan, scale),
+        out_shape=[
+            shape((n_patch, hidden)),
+            shape((hidden, n_patch)),
+            shape((hidden,)),
+            shape((width,)),
+            shape((width,)),
+        ],
+        in_specs=[VM] * len(args),
+        out_specs=[VM] * 5,
+        scratch_shapes=[
+            pltpu.VMEM((n_patch, hidden), BF16),
+        ],
+        name="last",
+        compiler_params=LIMIT,
+    )(*args)
     return jnp.swapaxes(final, 1, 2), dw_in, dw_out, db, d_gain, d_shift
 
 
@@ -642,21 +697,21 @@
         shape(x.shape, BF16),
         shape((images, width, hidden), BF16),
         shape((images, width, hidden), BF16),
-        shape(x.shape, BF16),
-        shape((1, hidden)),
+        shape((n_patch, hidden), BF16),
     ]
-    mr, normed, act, gp, gn, db = pl.pallas_call(
+    mr, normed, act, gp, send = pl.pallas_call(
         functools.partial(main_body, n_chan, channels),
         out_shape=outs,
         in_specs=[VM] * len(args),
         out_specs=[VM] * len(outs),
-        scratch_shapes=[pltpu.VMEM((width, hidden), F32)] * 4 + [pltpu.VMEM((8, hidden), F32)],
+        scratch_shapes=[pltpu.VMEM((width, hidden), F32)] * 4 + [pltpu.VMEM((n_patch, hidden), F32)],
         name="main",
         compiler_params=LIMIT,
     )(*args)
 
-    plan = role_plan if n_dp // 2 == n_chan else plain_plan
-    return plan(x, cot, mr, normed, act, gp, gn, db, gain, scale, channels)
+    roles = n_dp // 2 == n_chan and side_fits(images, n_patch, hidden)
+    plan = role_plan if roles else plain_plan
+    return plan(x, cot, mr, normed, act, gp, send, gain, w_token_in, scale, channels)
 
 
 def solution(mesh):

time: 48.9 us -> 46.1 us (0.943)
  waiting for transfers between devices: 14.7 us -> 12 us
    ppermute x7 -> x9, waiting for transfers between devices: 9.06 us -> 4.83 us  [exchange(): lax.ppermute(value, axis, [(i, i ^ j * stride) for i in range(n)])]
    pallas_call x10 -> x6, Pallas kernels: 4.51 us -> 1.92 us  [call(): pl.pallas_call(body, out_shape=outs, in_specs=[VM] * len(args), out_specs...]
    pallas_call x2 -> x4, Pallas kernels: 4.33 us -> 6.5 us  [the longest x1 1.93 us: back_call(): pl.pallas_call(back_body, out_shape=[shape(x.shape, BF16), shape((2 * ima...]
    ppermute x9, waiting for transfers between devices: 5.63 us -> 7.2 us  [role_exchange(): lax.ppermute(v, ('dp', 'chan'), role_pairs(n_dp, n_chan, j, swap))]
    ppermute x7 -> x9, starting transfers between devices: 6.11 us -> 5.92 us  [exchange(): lax.ppermute(value, axis, [(i, i ^ j * stride) for i in range(n)])]
  transfers between devices with their start and end apart: 16 -> 18, of which waited for: 10 -> 10; matrix products, arithmetic and copies ran while one was open for 0% -> 0% of each run, Pallas kernels for 12% -> 14%
where the time goes in v1:
time: 46.1 us; the launch traced here: 45.9 us
  starting transfers between devices  17.5 us (38%)
  Pallas kernels  13.7 us (30%)
  waiting for transfers between devices  12 us (26%)
  local copies, waits for them, and re-layouts  1.8 us (4%)
  between operations  0.84 us (2%)
    ppermute x9, starting transfers between devices, role_exchange(): lax.ppermute(v, ('dp', 'chan'), role_pairs(n_dp, n_chan, j, swap))  11.6 us
    ppermute x9, waiting for transfers between devices, role_exchange(): lax.ppermute(v, ('dp', 'chan'), role_pairs(n_dp, n_chan, j, swap))  7.2 us
    ppermute x9, starting transfers between devices, exchange(): lax.ppermute(value, axis, [(i, i ^ j * stride) for i in range(n)])  5.92 us
    pallas_call x1, Pallas kernels, shards(): pl.pallas_call(functools.partial(main_body, n_chan, channels), out_shape=...  5.31 us
    ppermute x9, waiting for transfers between devices, exchange(): lax.ppermute(value, axis, [(i, i ^ j * stride) for i in range(n)])  4.83 us
    pallas_call x1, Pallas kernels, back_call(): pl.pallas_call(back_body, out_shape=[shape(x.shape, BF16), shape((2 * ima...  1.93 us
    pallas_call x6, Pallas kernels, call(): pl.pallas_call(body, out_shape=outs, in_specs=[VM] * len(args), out_specs...  1.92 us
    unnamed x16, local copies, waits for them, and re-layouts  1.79 us
  transfers between devices with their start and end apart: 18, of which 10 were waited for; matrix products, arithmetic and copies ran while one was open for 0% of the time, Pallas kernels for 14%

profile of v1, /device:TPU:0, one launch (start us, length us, event | category | flops | bytes accessed | tf_op | source)
XLA Modules:
  0.0 45.9 jit_solution(14230569979041386610)
XLA Ops:
  0.6 0.0 copy-start
  0.6 1.3 %copy-done = bf16[8,256,320]{1,2,0:T(8,128)(2,1)S(1)} copy-done((bf16[8,256,320]{1,2,0:T(8,128)(2,1)S(1)}, bf16[8,256,320]{1,2,0:T(8,128)(2,1)}, u32[]{:S(2)}) %copy-start) | copy-done | bytes 1310744
  2.0 0.0 copy-start.5
  2.0 0.0 copy-start.6
  2.0 0.3 shard_map.118.refs_0_
  2.2 5.1 %collective-permute-start.2 = (f32[16,256]{1,0:T(8,128)S(1)}, f32[16,256]{1,0:T(8,128)S(1)}, u32[]{:S(2)}, u32[]{:S(2)}) collective-permute-start(f32[16,256]{1,0:T(8,128)S(1)} %shard_map.118.refs_0_), channel_id=1, source_target_pairs={{0,3},{1,2},{2,1},{3,0},{4,7},{5,6},{6,5},{7,4},{8,11},{9,10},{10,... | collective-permute-start | bytes 49160 | tf_op jit(solution)/shard_map/ppermute | solution.py:72
  7.4 0.0 collective-permute-start.1
  7.4 0.6 %collective-permute-start = (f32[16,256]{1,0:T(8,128)S(1)}, f32[16,256]{1,0:T(8,128)S(1)}, u32[]{:S(2)}, u32[]{:S(2)}) collective-permute-start(f32[16,256]{1,0:T(8,128)S(1)} %shard_map.118.refs_0_), channel_id=1, source_target_pairs={{0,1},{1,0},{2,3},{3,2},{4,5},{5,4},{6,7},{7,6},{8,9},{9,8},{10,11... | collective-permute-start | bytes 49160 | tf_op jit(solution)/shard_map/ppermute | solution.py:72
  8.0 0.0 copy-done.5
  8.0 0.0 copy-done.6
  8.0 0.0 copy-start.7
  8.0 0.0 copy-start.1
  8.1 0.0 copy-start.2
  8.1 0.0 copy-start.3
  8.1 0.0 copy-start.4
  8.1 0.2 shard_map.119
  8.3 0.4 copy-done.7
  8.7 0.4 collective-permute-done.2.refs_3_
  9.1 2.9 %collective-permute-done.1.refs_2_ = f32[16,256]{1,0:T(8,128)S(1)} collective-permute-done((f32[16,256]{1,0:T(8,128)S(1)}, f32[16,256]{1,0:T(8,128)S(1)}, u32[]{:S(2)}, u32[]{:S(2)}) %collective-permute-start.1) | collective-permute-done | bytes 16416 | tf_op jit(solution)/shard_map/ppermute | solution.py:72
  12.0 0.0 collective-permute-done.refs_1_
  12.0 0.0 copy-done.1
  12.0 0.0 copy-done.2
  12.0 0.0 copy-done.3
  12.0 0.0 copy-done.4
  12.0 5.3 %main.1 = (f32[2,8,256]{2,1,0:T(8,128)S(1)}, bf16[8,320,256]{2,1,0:T(8,128)(2,1)S(1)}, bf16[8,320,640]{2,1,0:T(8,128)(2,1)S(1)}, bf16[8,320,640]{2,1,0:T(8,128)(2,1)S(1)}, bf16[256,640]{1,0:T(8,128)(2,1)S(1)}) custom-call(bf16[8,320,256]{2,1,0:T(8,128)(2,1)S(1)} %bitcast.4, f32[16,256]{1,0:T(8,128)S(1)} %shard_map.118.refs_0_, ...), custom_call_target="tpu_custom_call" | custom-call | tf_op jit(solution)/shard_map/main/pallas_call | solution.py:702
  17.3 0.1 collective-permute-start.3
  17.4 1.2 %shard_map.120.own_ref = f32[256,640]{1,0:T(8,128)S(1)} custom-call(bf16[8,320,256]{2,1,0:T(8,128)(2,1)S(1)} %bitcast.9, bf16[8,320,640]{2,1,0:T(8,128)(2,1)S(1)} %get-tuple-element.30.act_ref, bf16[8,320,256]{2,1,0:T(8,128)(2,1)S(1)} %get-tuple-element.31.n_ref, bf16[8,320,640]{2,1,0:T(8,128)(2,1)S(1)} %get-tuple-element.28.gp_ref), custom_call_target="tpu_custom_call" | custom-call | flops 838860800 | bytes 9830400 | tf_op jit(solution)/shard_map/pallas_call | solution.py:25
  18.7 0.4 collective-permute-done.3.got_ref
  19.0 0.1 shard_map.121
  19.2 1.6 %collective-permute-start.4 = (bf16[64,640]{1,0:T(8,128)(2,1)S(1)}, bf16[64,640]{1,0:T(8,128)(2,1)S(1)}, u32[]{:S(2)}, u32[]{:S(2)}) collective-permute-start(bf16[64,640]{1,0:T(8,128)(2,1)S(1)} %get-tuple-element.36), channel_id=1, source_target_pairs={{0,8},{1,9},{2,10},{3,11},{4,5},{5,4},{6,7},{7,6},{8,0},{9,1},{10,... | collective-permute-start | bytes 245768 | tf_op jit(solution)/shard_map/ppermute | solution.py:460
  20.7 1.5 %collective-permute-start.5 = (bf16[64,640]{1,0:T(8,128)(2,1)S(1)}, bf16[64,640]{1,0:T(8,128)(2,1)S(1)}, u32[]{:S(2)}, u32[]{:S(2)}) collective-permute-start(bf16[64,640]{1,0:T(8,128)(2,1)S(1)} %get-tuple-element.37), channel_id=1, source_target_pairs={{0,16},{1,17},{2,18},{3,19},{4,6},{5,7},{6,4},{7,5},{8,24},{9,25},... | collective-permute-start | bytes 245768 | tf_op jit(solution)/shard_map/ppermute | solution.py:460
  22.3 0.5 %collective-permute-start.6 = (bf16[64,640]{1,0:T(8,128)(2,1)S(1)}, bf16[64,640]{1,0:T(8,128)(2,1)S(1)}, u32[]{:S(2)}, u32[]{:S(2)}) collective-permute-start(bf16[64,640]{1,0:T(8,128)(2,1)S(1)} %get-tuple-element.38), channel_id=1, source_target_pairs={{0,24},{1,25},{2,26},{3,27},{4,7},{5,6},{6,5},{7,4},{8,16},{9,17},... | collective-permute-start | bytes 245768 | tf_op jit(solution)/shard_map/ppermute | solution.py:460
  22.7 1.9 %back.1 = (bf16[8,320,256]{2,1,0:T(8,128)(2,1)S(1)}, f32[16,256]{1,0:T(8,128)S(1)}, f32[1,640]{1,0:T(1,128)S(1)}) custom-call(bf16[8,320,256]{2,1,0:T(8,128)(2,1)S(1)} %bitcast.5, f32[2,8,256]{2,1,0:T(8,128)S(1)} %get-tuple-element.27.mr_ref, f32[320,256]{1,0:T(8,128)S(1)} %get-tuple-element.25.refs_4_.gain_ref, ...), custom_call_target="tpu_custom_call" | custom-call | flops 1073741824 | bytes 4194304 | tf_op jit(solution)/shard_map/back/pallas_call | solution.py:252
  24.7 0.0 collective-permute-done.4.refs_0_
  24.7 0.5 %collective-permute-done.5.refs_1_ = bf16[64,640]{1,0:T(8,128)(2,1)S(1)} collective-permute-done((bf16[64,640]{1,0:T(8,128)(2,1)S(1)}, bf16[64,640]{1,0:T(8,128)(2,1)S(1)}, u32[]{:S(2)}, u32[]{:S(2)}) %collective-permute-start.5) | collective-permute-done | bytes 81952 | tf_op jit(solution)/shard_map/ppermute | solution.py:460
  25.2 2.4 %collective-permute-done.6.refs_2_ = bf16[64,640]{1,0:T(8,128)(2,1)S(1)} collective-permute-done((bf16[64,640]{1,0:T(8,128)(2,1)S(1)}, bf16[64,640]{1,0:T(8,128)(2,1)S(1)}, u32[]{:S(2)}, u32[]{:S(2)}) %collective-permute-start.6) | collective-permute-done | bytes 81952 | tf_op jit(solution)/shard_map/ppermute | solution.py:460
  27.6 1.7 %collective-permute-start.9 = (bf16[72,640]{1,0:T(8,128)(2,1)S(1)}, bf16[72,640]{1,0:T(8,128)(2,1)S(1)}, u32[]{:S(2)}, u32[]{:S(2)}) collective-permute-start(bf16[72,640]{1,0:T(8,128)(2,1)S(1)} %shard_map.122.refs_0_), channel_id=1, source_target_pairs={{0,3},{1,2},{2,1},{3,0},{4,28},{5,29},{6,30},{7,31},{8,11},{9,10},... | collective-permute-start | bytes 276488 | tf_op jit(solution)/shard_map/ppermute | solution.py:460
  29.3 0.5 %collective-permute-start.8 = (bf16[72,640]{1,0:T(8,128)(2,1)S(1)}, bf16[72,640]{1,0:T(8,128)(2,1)S(1)}, u32[]{:S(2)}, u32[]{:S(2)}) collective-permute-start(bf16[72,640]{1,0:T(8,128)(2,1)S(1)} %shard_map.122.refs_0_), channel_id=1, source_target_pairs={{0,2},{1,3},{2,0},{3,1},{4,20},{5,21},{6,22},{7,23},{8,10},{9,11},... | collective-permute-start | bytes 276488 | tf_op jit(solution)/shard_map/ppermute | solution.py:460
  29.8 2.3 %collective-permute-start.7 = (bf16[72,640]{1,0:T(8,128)(2,1)S(1)}, bf16[72,640]{1,0:T(8,128)(2,1)S(1)}, u32[]{:S(2)}, u32[]{:S(2)}) collective-permute-start(bf16[72,640]{1,0:T(8,128)(2,1)S(1)} %shard_map.122.refs_0_), channel_id=1, source_target_pairs={{0,1},{1,0},{2,3},{3,2},{4,12},{5,13},{6,14},{7,15},{8,9},{9,8},{1... | collective-permute-start | bytes 276488 | tf_op jit(solution)/shard_map/ppermute | solution.py:460
  32.1 1.5 %norm.1.norm_ref = f32[1,640]{1,0:T(1,128)S(1)} custom-call(bf16[8,320,256]{2,1,0:T(8,128)(2,1)S(1)} %bitcast.6, f32[2,8,256]{2,1,0:T(8,128)S(1)} %get-tuple-element.27.mr_ref, bf16[8,320,256]{2,1,0:T(8,128)(2,1)S(1)} %get-tuple-element.29.gn_ref), custom_call_target="tpu_custom_call" | custom-call | flops 536870912 | bytes 4194304 | tf_op jit(solution)/shard_map/norm/pallas_call | solution.py:367
  33.6 0.0 collective-permute-start.10
  33.6 1.2 %collective-permute-done.10.norm_got_ref = f32[1,640]{1,0:T(1,128)S(1)} collective-permute-done((f32[1,640]{1,0:T(1,128)S(1)}, f32[1,640]{1,0:T(1,128)S(1)}, u32[]{:S(2)}, u32[]{:S(2)}) %collective-permute-start.10) | collective-permute-done | bytes 2592 | tf_op jit(solution)/shard_map/ppermute | solution.py:72
  34.7 0.0 collective-permute-done.9.refs_3_
  34.8 1.3 %collective-permute-done.8.refs_2_ = bf16[72,640]{1,0:T(8,128)(2,1)S(1)} collective-permute-done((bf16[72,640]{1,0:T(8,128)(2,1)S(1)}, bf16[72,640]{1,0:T(8,128)(2,1)S(1)}, u32[]{:S(2)}, u32[]{:S(2)}) %collective-permute-start.8) | collective-permute-done | bytes 92192 | tf_op jit(solution)/shard_map/ppermute | solution.py:460
  36.0 0.0 collective-permute-done.7.refs_1_
  36.0 0.1 shard_map.123.refs_4_.refs_0_
  36.1 0.5 %collective-permute-start.13 = (bf16[72,640]{1,0:T(8,128)(2,1)S(1)}, bf16[72,640]{1,0:T(8,128)(2,1)S(1)}, u32[]{:S(2)}, u32[]{:S(2)}) collective-permute-start(bf16[72,640]{1,0:T(8,128)(2,1)S(1)} %shard_map.123.refs_4_.refs_0_), channel_id=1, source_target_pairs={{0,24},{1,25},{2,26},{3,27},{4,7},{5,6},{6,5},{7,4},{8,16},{9,17},... | collective-permute-start | bytes 276488 | tf_op jit(solution)/shard_map/ppermute | solution.py:460
  36.7 1.5 %collective-permute-start.12 = (bf16[72,640]{1,0:T(8,128)(2,1)S(1)}, bf16[72,640]{1,0:T(8,128)(2,1)S(1)}, u32[]{:S(2)}, u32[]{:S(2)}) collective-permute-start(bf16[72,640]{1,0:T(8,128)(2,1)S(1)} %shard_map.123.refs_4_.refs_0_), channel_id=1, source_target_pairs={{0,16},{1,17},{2,18},{3,19},{4,6},{5,7},{6,4},{7,5},{8,24},{9,25},... | collective-permute-start | bytes 276488 | tf_op jit(solution)/shard_map/ppermute | solution.py:460
  38.2 1.5 %collective-permute-start.11 = (bf16[72,640]{1,0:T(8,128)(2,1)S(1)}, bf16[72,640]{1,0:T(8,128)(2,1)S(1)}, u32[]{:S(2)}, u32[]{:S(2)}) collective-permute-start(bf16[72,640]{1,0:T(8,128)(2,1)S(1)} %shard_map.123.refs_4_.refs_0_), channel_id=1, source_target_pairs={{0,8},{1,9},{2,10},{3,11},{4,5},{5,4},{6,7},{7,6},{8,0},{9,1},{10,... | collective-permute-start | bytes 276488 | tf_op jit(solution)/shard_map/ppermute | solution.py:460
  39.7 0.0 collective-permute-start.14
  39.7 2.1 %collective-permute-done.13.refs_7_.refs_3_ = bf16[72,640]{1,0:T(8,128)(2,1)S(1)} collective-permute-done((bf16[72,640]{1,0:T(8,128)(2,1)S(1)}, bf16[72,640]{1,0:T(8,128)(2,1)S(1)}, u32[]{:S(2)}, u32[]{:S(2)}) %collective-permute-start.13) | collective-permute-done | bytes 92192 | tf_op jit(solution)/shard_map/ppermute | solution.py:460
  41.7 0.0 collective-permute-start.17
  41.7 0.5 collective-permute-done.12.refs_6_.refs_2_
  42.2 0.1 collective-permute-start.16
  42.2 0.5 %collective-permute-done.11.refs_5_.refs_1_ = bf16[72,640]{1,0:T(8,128)(2,1)S(1)} collective-permute-done((bf16[72,640]{1,0:T(8,128)(2,1)S(1)}, bf16[72,640]{1,0:T(8,128)(2,1)S(1)}, u32[]{:S(2)}, u32[]{:S(2)}) %collective-permute-start.11) | collective-permute-done | bytes 92192 | tf_op jit(solution)/shard_map/ppermute | solution.py:460
  42.7 0.0 collective-permute-start.15
  42.7 1.8 %input.1 = bf16[8,320,256]{2,1,0:T(8,128)(2,1)} custom-call(bf16[8,320,256]{2,1,0:T(8,128)(2,1)S(1)} %bitcast.7, bf16[8,320,256]{2,1,0:T(8,128)(2,1)S(1)} %bitcast.10, bf16[8,320,256]{2,1,0:T(8,128)(2,1)S(1)} %get-tuple-element.29.gn_ref, f32[2,8,256]{2,1,0:T(8,128)S(1)} %get-tuple-element.27.mr_ref, f32[320,256]{1,0:T(8,128)S(1)} %get-tuple-element.25.refs_4_.gain_ref, ...), custom_call_target="tpu_custom_call" | custom-call | flops 838860800 | bytes 4194304 | tf_op jit(solution)/shard_map/input/pallas_call | solution.py:637
  44.5 0.0 collective-permute-done.14.refs_4_
  44.5 0.0 collective-permute-done.17.refs_7_
  44.5 0.0 collective-permute-done.16.refs_6_
  44.5 0.0 collective-permute-done.15.refs_5_
  44.5 1.3 %last.1 = (f32[256,640]{1,0:T(8,128)}, f32[640,256]{1,0:T(8,128)}, f32[640]{0:T(1024)}, f32[320]{0:T(512)}, f32[320]{0:T(512)}) custom-call(bf16[72,640]{1,0:T(8,128)(2,1)S(1)} %shard_map.123.refs_4_.refs_0_, bf16[72,640]{1,0:T(8,128)(2,1)S(1)} %collective-permute-done.11.refs_5_.refs_1_, bf16[72,640]{1,0:T(8,128)(2,1)S(1)} %collective-permute-done.12.refs_6_.refs_2_, ...), custom_call_target="tpu_custom_call" | custom-call | tf_op jit(solution)/shard_map/last/pallas_call | solution.py:655
  (4 shorter events, 0.1 us)
Async XLA Ops:
  0.6 1.3 %copy-start = (bf16[8,256,320]{1,2,0:T(8,128)(2,1)S(1)}, bf16[8,256,320]{1,2,0:T(8,128)(2,1)}, u32[]{:S(2)}) copy-start(bf16[8,256,320]{1,2,0:T(8,128)(2,1)} %param.7) | copy-start | bytes 3932164
  2.0 6.1 %copy-start.5 = (f32[1280]{0:T(1024)S(1)}, f32[1280]{0:T(1024)}, u32[]{:S(2)}) copy-start(f32[1280]{0:T(1024)} %param.12) | copy-start | bytes 15364
  2.0 6.1 %copy-start.6 = (f32[1280]{0:T(1024)S(1)}, f32[1280]{0:T(1024)}, u32[]{:S(2)}) copy-start(f32[1280]{0:T(1024)} %param.13) | copy-start | bytes 15364
  2.2 6.9 %collective-permute-start.2 = (f32[16,256]{1,0:T(8,128)S(1)}, f32[16,256]{1,0:T(8,128)S(1)}, u32[]{:S(2)}, u32[]{:S(2)}) collective-permute-start(f32[16,256]{1,0:T(8,128)S(1)} %shard_map.118.refs_0_), channel_id=1, source_target_pairs={{0,3},{1,2},{2,1},{3,0},{4,7},{5,6},{6,5},{7,4},{8,11},{9,10},{10,... | collective-permute-start | bytes 49160 | tf_op jit(solution)/shard_map/ppermute | solution.py:72
  7.4 4.6 %collective-permute-start.1 = (f32[16,256]{1,0:T(8,128)S(1)}, f32[16,256]{1,0:T(8,128)S(1)}, u32[]{:S(2)}, u32[]{:S(2)}) collective-permute-start(f32[16,256]{1,0:T(8,128)S(1)} %shard_map.118.refs_0_), channel_id=1, source_target_pairs={{0,2},{1,3},{2,0},{3,1},{4,6},{5,7},{6,4},{7,5},{8,10},{9,11},{10,... | collective-permute-start | bytes 49160 | tf_op jit(solution)/shard_map/ppermute | solution.py:72
  7.4 4.6 %collective-permute-start = (f32[16,256]{1,0:T(8,128)S(1)}, f32[16,256]{1,0:T(8,128)S(1)}, u32[]{:S(2)}, u32[]{:S(2)}) collective-permute-start(f32[16,256]{1,0:T(8,128)S(1)} %shard_map.118.refs_0_), channel_id=1, source_target_pairs={{0,1},{1,0},{2,3},{3,2},{4,5},{5,4},{6,7},{7,6},{8,9},{9,8},{10,11... | collective-permute-start | bytes 49160 | tf_op jit(solution)/shard_map/ppermute | solution.py:72
  8.0 0.7 %copy-start.7 = (f32[640]{0:T(1024)S(1)}, f32[640]{0:T(1024)}, u32[]{:S(2)}) copy-start(f32[640]{0:T(1024)} %param.10) | copy-start | bytes 7684
  8.0 4.0 %copy-start.1 = (bf16[8,256,320]{1,2,0:T(8,128)(2,1)S(1)}, bf16[8,256,320]{1,2,0:T(8,128)(2,1)}, u32[]{:S(2)}) copy-start(bf16[8,256,320]{1,2,0:T(8,128)(2,1)} %param.7) | copy-start | bytes 3932164
  8.1 4.0 %copy-start.2 = (bf16[8,256,320]{1,2,0:T(8,128)(2,1)S(1)}, bf16[8,256,320]{1,2,0:T(8,128)(2,1)}, u32[]{:S(2)}) copy-start(bf16[8,256,320]{1,2,0:T(8,128)(2,1)} %param.8) | copy-start | bytes 3932164
  8.1 3.9 %copy-start.3 = (bf16[640,256]{1,0:T(8,128)(2,1)S(1)}, bf16[640,256]{1,0:T(8,128)(2,1)}, u32[]{:S(2)}) copy-start(bf16[640,256]{1,0:T(8,128)(2,1)} %w_ref.1) | copy-start | bytes 983044
  8.1 3.9 %copy-start.4 = (bf16[256,640]{1,0:T(8,128)(2,1)S(1)}, bf16[256,640]{1,0:T(8,128)(2,1)}, u32[]{:S(2)}) copy-start(bf16[256,640]{1,0:T(8,128)(2,1)} %refs_9_.1) | copy-start | bytes 983044
  17.3 1.7 %collective-permute-start.3 = (bf16[256,640]{1,0:T(8,128)(2,1)S(1)}, bf16[256,640]{1,0:T(8,128)(2,1)S(1)}, u32[]{:S(2)}, u32[]{:S(2)}) collective-permute-start(bf16[256,640]{1,0:T(8,128)(2,1)S(1)} %get-tuple-element.32), channel_id=1, source_target_pairs={{0,4},{4,0},{8,12},{12,8},{16,20},{20,16},{24,28},{28,24},{1,5},{5... | collective-permute-start | bytes 983048 | tf_op jit(solution)/shard_map/ppermute | solution.py:72
  19.2 5.5 %collective-permute-start.4 = (bf16[64,640]{1,0:T(8,128)(2,1)S(1)}, bf16[64,640]{1,0:T(8,128)(2,1)S(1)}, u32[]{:S(2)}, u32[]{:S(2)}) collective-permute-start(bf16[64,640]{1,0:T(8,128)(2,1)S(1)} %get-tuple-element.36), channel_id=1, source_target_pairs={{0,8},{1,9},{2,10},{3,11},{4,5},{5,4},{6,7},{7,6},{8,0},{9,1},{10,... | collective-permute-start | bytes 245768 | tf_op jit(solution)/shard_map/ppermute | solution.py:460
  20.7 4.4 %collective-permute-start.5 = (bf16[64,640]{1,0:T(8,128)(2,1)S(1)}, bf16[64,640]{1,0:T(8,128)(2,1)S(1)}, u32[]{:S(2)}, u32[]{:S(2)}) collective-permute-start(bf16[64,640]{1,0:T(8,128)(2,1)S(1)} %get-tuple-element.37), channel_id=1, source_target_pairs={{0,16},{1,17},{2,18},{3,19},{4,6},{5,7},{6,4},{7,5},{8,24},{9,25},... | collective-permute-start | bytes 245768 | tf_op jit(solution)/shard_map/ppermute | solution.py:460
  22.3 5.3 %collective-permute-start.6 = (bf16[64,640]{1,0:T(8,128)(2,1)S(1)}, bf16[64,640]{1,0:T(8,128)(2,1)S(1)}, u32[]{:S(2)}, u32[]{:S(2)}) collective-permute-start(bf16[64,640]{1,0:T(8,128)(2,1)S(1)} %get-tuple-element.38), channel_id=1, source_target_pairs={{0,24},{1,25},{2,26},{3,27},{4,7},{5,6},{6,5},{7,4},{8,16},{9,17},... | collective-permute-start | bytes 245768 | tf_op jit(solution)/shard_map/ppermute | solution.py:460
  27.6 7.1 %collective-permute-start.9 = (bf16[72,640]{1,0:T(8,128)(2,1)S(1)}, bf16[72,640]{1,0:T(8,128)(2,1)S(1)}, u32[]{:S(2)}, u32[]{:S(2)}) collective-permute-start(bf16[72,640]{1,0:T(8,128)(2,1)S(1)} %shard_map.122.refs_0_), channel_id=1, source_target_pairs={{0,3},{1,2},{2,1},{3,0},{4,28},{5,29},{6,30},{7,31},{8,11},{9,10},... | collective-permute-start | bytes 276488 | tf_op jit(solution)/shard_map/ppermute | solution.py:460
  29.3 6.7 %collective-permute-start.8 = (bf16[72,640]{1,0:T(8,128)(2,1)S(1)}, bf16[72,640]{1,0:T(8,128)(2,1)S(1)}, u32[]{:S(2)}, u32[]{:S(2)}) collective-permute-start(bf16[72,640]{1,0:T(8,128)(2,1)S(1)} %shard_map.122.refs_0_), channel_id=1, source_target_pairs={{0,2},{1,3},{2,0},{3,1},{4,20},{5,21},{6,22},{7,23},{8,10},{9,11},... | collective-permute-start | bytes 276488 | tf_op jit(solution)/shard_map/ppermute | solution.py:460
  29.8 6.2 %collective-permute-start.7 = (bf16[72,640]{1,0:T(8,128)(2,1)S(1)}, bf16[72,640]{1,0:T(8,128)(2,1)S(1)}, u32[]{:S(2)}, u32[]{:S(2)}) collective-permute-start(bf16[72,640]{1,0:T(8,128)(2,1)S(1)} %shard_map.122.refs_0_), channel_id=1, source_target_pairs={{0,1},{1,0},{2,3},{3,2},{4,12},{5,13},{6,14},{7,15},{8,9},{9,8},{1... | collective-permute-start | bytes 276488 | tf_op jit(solution)/shard_map/ppermute | solution.py:460
  33.6 1.2 %collective-permute-start.10 = (f32[1,640]{1,0:T(1,128)S(1)}, f32[1,640]{1,0:T(1,128)S(1)}, u32[]{:S(2)}, u32[]{:S(2)}) collective-permute-start(f32[1,640]{1,0:T(1,128)S(1)} %norm.1.norm_ref), channel_id=1, source_target_pairs={{0,4},{4,0},{8,12},{12,8},{16,20},{20,16},{24,28},{28,24},{1,5},{5... | collective-permute-start | bytes 7688 | tf_op jit(solution)/shard_map/ppermute | solution.py:72
  36.1 5.6 %collective-permute-start.13 = (bf16[72,640]{1,0:T(8,128)(2,1)S(1)}, bf16[72,640]{1,0:T(8,128)(2,1)S(1)}, u32[]{:S(2)}, u32[]{:S(2)}) collective-permute-start(bf16[72,640]{1,0:T(8,128)(2,1)S(1)} %shard_map.123.refs_4_.refs_0_), channel_id=1, source_target_pairs={{0,24},{1,25},{2,26},{3,27},{4,7},{5,6},{6,5},{7,4},{8,16},{9,17},... | collective-permute-start | bytes 276488 | tf_op jit(solution)/shard_map/ppermute | solution.py:460
  36.7 5.5 %collective-permute-start.12 = (bf16[72,640]{1,0:T(8,128)(2,1)S(1)}, bf16[72,640]{1,0:T(8,128)(2,1)S(1)}, u32[]{:S(2)}, u32[]{:S(2)}) collective-permute-start(bf16[72,640]{1,0:T(8,128)(2,1)S(1)} %shard_map.123.refs_4_.refs_0_), channel_id=1, source_target_pairs={{0,16},{1,17},{2,18},{3,19},{4,6},{5,7},{6,4},{7,5},{8,24},{9,25},... | collective-permute-start | bytes 276488 | tf_op jit(solution)/shard_map/ppermute | solution.py:460
  38.2 4.6 %collective-permute-start.11 = (bf16[72,640]{1,0:T(8,128)(2,1)S(1)}, bf16[72,640]{1,0:T(8,128)(2,1)S(1)}, u32[]{:S(2)}, u32[]{:S(2)}) collective-permute-start(bf16[72,640]{1,0:T(8,128)(2,1)S(1)} %shard_map.123.refs_4_.refs_0_), channel_id=1, source_target_pairs={{0,8},{1,9},{2,10},{3,11},{4,5},{5,4},{6,7},{7,6},{8,0},{9,1},{10,... | collective-permute-start | bytes 276488 | tf_op jit(solution)/shard_map/ppermute | solution.py:460
  39.7 4.8 %collective-permute-start.14 = (bf16[72,640]{1,0:T(8,128)(2,1)S(1)}, bf16[72,640]{1,0:T(8,128)(2,1)S(1)}, u32[]{:S(2)}, u32[]{:S(2)}) collective-permute-start(bf16[72,640]{1,0:T(8,128)(2,1)S(1)} %shard_map.123.refs_4_.refs_0_), channel_id=1, source_target_pairs={{0,4},{4,0},{8,12},{12,8},{16,20},{20,16},{24,28},{28,24},{1,5},{5... | collective-permute-start | bytes 276488 | tf_op jit(solution)/shard_map/ppermute | solution.py:72
  41.7 2.8 %collective-permute-start.17 = (bf16[72,640]{1,0:T(8,128)(2,1)S(1)}, bf16[72,640]{1,0:T(8,128)(2,1)S(1)}, u32[]{:S(2)}, u32[]{:S(2)}) collective-permute-start(bf16[72,640]{1,0:T(8,128)(2,1)S(1)} %collective-permute-done.13.refs_7_.refs_3_), channel_id=1, source_target_pairs={{0,4},{4,0},{8,12},{12,8},{16,20},{20,16},{24,28},{28,24},{1,5},{5... | collective-permute-start | bytes 276488 | tf_op jit(solution)/shard_map/ppermute | solution.py:72
  42.2 2.3 %collective-permute-start.16 = (bf16[72,640]{1,0:T(8,128)(2,1)S(1)}, bf16[72,640]{1,0:T(8,128)(2,1)S(1)}, u32[]{:S(2)}, u32[]{:S(2)}) collective-permute-start(bf16[72,640]{1,0:T(8,128)(2,1)S(1)} %collective-permute-done.12.refs_6_.refs_2_), channel_id=1, source_target_pairs={{0,4},{4,0},{8,12},{12,8},{16,20},{20,16},{24,28},{28,24},{1,5},{5... | collective-permute-start | bytes 276488 | tf_op jit(solution)/shard_map/ppermute | solution.py:72
  42.7 1.8 %collective-permute-start.15 = (bf16[72,640]{1,0:T(8,128)(2,1)S(1)}, bf16[72,640]{1,0:T(8,128)(2,1)S(1)}, u32[]{:S(2)}, u32[]{:S(2)}) collective-permute-start(bf16[72,640]{1,0:T(8,128)(2,1)S(1)} %collective-permute-done.11.refs_5_.refs_1_), channel_id=1, source_target_pairs={{0,4},{4,0},{8,12},{12,8},{16,20},{20,16},{24,28},{28,24},{1,5},{5... | collective-permute-start | bytes 276488 | tf_op jit(solution)/shard_map/ppermute | solution.py:72
